TPU v7x, 1024 devices: a whole 4x4x32 slice. The times are simulated.
1024 devices in a mesh: ctx: 128 (over z, x_hi, core), fsdp: 8 (over y, x_lo).
Axes of the slice: x: 4 (x_hi: 2, x_lo: 2; x = x_hi * 2 + x_lo), y: 4, z: 32, core: 2. Of those that a mesh axis runs over, the one named last changes fastest.
Arguments:
- queries: bfloat16 [65536, 2048], P('ctx', 'fsdp'), may hold values from -30 to 30
- keys: bfloat16 [65536, 2048], P('ctx', 'fsdp'), may hold values from -10 to 10
- values: bfloat16 [65536, 2048], P('ctx', 'fsdp'), may hold values from -16 to 16
- norm_gain: float32 [2048], P('fsdp'), may hold values from 0.25 to 1.75
- short_filters: float32 [3, 3, 2048], P(None, None, 'fsdp'), may hold values from -3 to 3
- medium_filters: bfloat16 [128, 128], P(None, 'fsdp'), may hold values from -0.5 to 0.5
Outputs:
- mixed: bfloat16 [65536, 2048], P('ctx', 'fsdp')
All inputs are finite; a program needn't handle non-finite values.
Results may differ from a plain program's by a relative error of at most 0.012.
Values may be sent and summed in bfloat16 or wider, within the bound.
No kernel may reach another device: no remote copies, remote signals or barrier semaphores. Data moves between devices by JAX's collectives and lax.ppermute only.
A program may use at most 32 MiB of HBM per device.

v0:
```python
import functools
import math

import jax
import jax.numpy as jnp
from jax import lax
from jax.experimental import pallas as pl
from jax.experimental.pallas import tpu as pltpu
from jax.sharding import PartitionSpec as P


HEAD_DIM = 128
BLOCK = 256
HALO = 144
NEG = -1e30
EPS = 1e-6
LOG2E = 1.4426950408889634
SCALE = LOG2E / math.sqrt(HEAD_DIM)
VMEM = pl.BlockSpec(memory_space=pltpu.VMEM)
HBM = pl.BlockSpec(memory_space=pltpu.HBM)
HIGHEST = lax.Precision.HIGHEST
F32 = jnp.float32
BF16 = jnp.bfloat16


def cols_of(h):
    return slice(h * HEAD_DIM, (h + 1) * HEAD_DIM)


def peak_of(unit):
    q, groups, state = unit
    rows = q.shape[0]
    scores = []
    peak = None
    for pieces, gone in groups:
        top = None
        for k, v, mask in pieces:
            s = lax.dot_general(q, k, (((1,), (1,)), ((), ())), preferred_element_type=F32)
            if mask is not None:
                s = jnp.where(mask, s, NEG)
            scores.append((s, v, gone))
            for w in range(0, BLOCK, 128):
                piece = s[:, w : w + 128]
                top = piece if top is None else jnp.maximum(top, piece)
        if gone is not None:
            top = top - gone
        peak = top if peak is None else jnp.maximum(peak, top)
    peak = jnp.broadcast_to(jnp.max(peak, axis=1, keepdims=True), (rows, 128))
    if state is not None:
        peak = jnp.maximum(state[0], peak)
    return scores, peak


def weigh(unit, scores, peak):
    total = acc = None
    if unit[2] is not None:
        before, total, acc = unit[2]
        shrink = jnp.exp2((before - peak) * SCALE)
        total, acc = total * shrink, acc * shrink
    for s, v, gone in scores:
        off = peak if gone is None else peak + gone
        halves = []
        for w in range(0, BLOCK, 128):
            p = jnp.exp2((s[:, w : w + 128] - off) * SCALE)
            total = p if total is None else total + p
            halves.append(p.astype(BF16))
        o = jnp.dot(jnp.concatenate(halves, axis=1), v, preferred_element_type=F32)
        acc = o if acc is None else acc + o
    return peak, total, acc


def run_units(units, done):
    ahead = peak_of(units[0][0])
    for i, (unit, tag) in enumerate(units):
        now = ahead
        if i + 1 < len(units):
            ahead = peak_of(units[i + 1][0])
        done(tag, weigh(unit, *now))


def finish(state):
    _, total, acc = state
    return (acc / jnp.sum(total, axis=1, keepdims=True)).astype(BF16)


def part(i):
    return slice(i * BLOCK, (i + 1) * BLOCK)


def grid_iota():
    shape = (BLOCK, BLOCK)
    return lax.broadcasted_iota(jnp.int32, shape, 0), lax.broadcasted_iota(jnp.int32, shape, 1)


def absent(distance):
    return jnp.where(lax.axis_index("ctx") >= distance, 0.0, -NEG).astype(F32)


def is_even():
    return lax.rem(lax.axis_index("ctx"), 2) == 0


def early_kernel(
    q_ref, k_ref, v_ref, filt_ref, short_ref, gain_ref, peak_ref, total_ref, acc_ref, table_ref,
    coef_ref,
):
    rows, channels = q_ref.shape
    ri, ci = grid_iota()
    units = []
    for h in range(channels // HEAD_DIM):
        cols = cols_of(h)
        for b in range(rows // BLOCK):
            pieces = [
                (k_ref[part(j), cols], v_ref[part(j), cols], ci <= ri if j == b else None)
                for j in range(b + 1)
            ]
            units.append(((q_ref[part(b), cols], [(pieces, None)], None), (part(b), cols)))

    def done(tag, state):
        peak_ref[tag], total_ref[tag], acc_ref[tag] = state

    run_units(units, done)
    groups, taps = filt_ref.shape
    tap = lax.broadcasted_iota(jnp.int32, (taps, 2 * taps), 0)
    ext = lax.broadcasted_iota(jnp.int32, (taps, 2 * taps), 1)
    flip = jnp.where(ext == taps - tap, 1.0, 0.0).astype(BF16)
    base = jnp.dot(filt_ref[...], flip, preferred_element_type=F32)
    for g in range(groups):
        row = jnp.broadcast_to(base[g : g + 1, :], (taps, 2 * taps))
        shifted = pltpu.roll(row, 0, 1, stride=1, stride_axis=0)
        table_ref[g * taps : (g + 1) * taps, :] = shifted.astype(BF16)
    for i in range(9):
        coef_ref[i : i + 1, :] = short_ref[i // 3, i % 3 : i % 3 + 1, :]
    coef_ref[9:10, :] = gain_ref[...]


def pick_keys_kernel(own_ref, far_ref, out_ref):
    rows = own_ref.shape[0]

    @pl.when(is_even())
    def _():
        out_ref[:rows, :] = own_ref[...]
        out_ref[rows:, :] = far_ref[rows - BLOCK :, :]

    @pl.when(jnp.logical_not(is_even()))
    def _():
        out_ref[:rows, :] = far_ref[...]


def pick_values_kernel(own_ref, far_ref, after_ref, out_ref):
    size = own_ref.shape[0]
    rows = size - HALO

    @pl.when(is_even())
    def _():
        out_ref[:size, :] = own_ref[...]
        out_ref[size:, :] = far_ref[rows - BLOCK : rows, :]

    @pl.when(jnp.logical_not(is_even()))
    def _():
        out_ref[:size, :] = far_ref[...]


def far_kernel(q_ref, k_ref, v_ref, peak_in, total_in, acc_in, peak_ref, total_ref, acc_ref):
    rows, channels = q_ref.shape
    blocks = rows // BLOCK
    gone = absent(2)
    ri, ci = grid_iota()
    units = []
    for h in range(channels // HEAD_DIM):
        cols = cols_of(h)
        for b in range(blocks):
            tag = (part(b), cols)
            pieces = [
                (k_ref[part(j), cols], v_ref[part(j), cols], ci > ri if j == b else None)
                for j in range(b, blocks)
            ]
            state = (peak_in[tag], total_in[tag], acc_in[tag])
            units.append(((q_ref[tag], [(pieces, gone)], state), tag))

    def done(tag, state):
        peak_ref[tag], total_ref[tag], acc_ref[tag] = state

    run_units(units, done)


def row_squares(att):
    af = att.astype(F32)
    af = af * af
    high = af.astype(BF16)
    low = (af - high.astype(F32)).astype(BF16)
    ones = jnp.ones((8, af.shape[1]), BF16)
    dims = (((1,), (1,)), ((), ()))
    return lax.dot_general(ones, high, dims, preferred_element_type=F32) + lax.dot_general(
        ones, low, dims, preferred_element_type=F32
    )


def near_kernel(
    q_ref, k2_ref, v2_ref, k1_ref, v1_ref, tails_ref, peak_in, total_in, acc_in,
    out_ref, halo_ref, sq_ref,
):
    rows, channels = q_ref.shape
    heads = channels // HEAD_DIM
    blocks = rows // BLOCK
    shift = BLOCK - HALO
    ri = lax.broadcasted_iota(jnp.int32, (HALO, BLOCK), 0)
    ci = lax.broadcasted_iota(jnp.int32, (HALO, BLOCK), 1)
    sq_ref[:, 0, :BLOCK] = jnp.zeros((sq_ref.shape[0], BLOCK), F32)
    units = []
    for h in range(heads):
        cols = cols_of(h)
        k3 = jnp.where(is_even(), tails_ref[:BLOCK, cols], k1_ref[rows:, cols])
        v3 = jnp.where(is_even(), tails_ref[BLOCK:, cols], v1_ref[rows + HALO :, cols])
        near = [(k1_ref[part(j), cols], v1_ref[part(j), cols], None) for j in range(blocks)]
        near[-1] = (*near[-1][:2], ci <= ri + shift)
        middle = [(k2_ref[part(j), cols], v2_ref[part(j), cols], None) for j in range(blocks)]
        groups = [
            (near, absent(1)),
            (middle, absent(2)),
            ([(k3, v3, ci > ri + shift)], absent(3)),
        ]
        units.append(((v1_ref[rows : rows + HALO, cols], groups, None), (None, h)))
    for b in range(blocks):
        for h in range(heads):
            cols = cols_of(h)
            tag = (part(b), cols)
            near = [(k1_ref[part(j), cols], v1_ref[part(j), cols], None) for j in range(blocks)]
            state = (peak_in[tag], total_in[tag], acc_in[tag])
            units.append(((q_ref[tag], [(near, absent(1))], state), (b, h)))

    def done(tag, state):
        b, h = tag
        att = finish(state)
        if b is None:
            halo_ref[:, cols_of(h)] = jnp.where(
                lax.axis_index("ctx") >= 1, att, jnp.zeros(att.shape, BF16)
            )
            if h == heads - 1:
                sq_ref[:, 0, :HALO] = row_squares(halo_ref[...])
        else:
            out_ref[part(b), cols_of(h)] = att
            if h == heads - 1:
                sq_ref[:, 0, part(b + 1)] = row_squares(out_ref[part(b), :])

    run_units(units, done)


def mix_kernel(total_channels, sq_ref, halo_ref, att_ref, coef_ref, table_ref, out_ref, ext_ref, prod_ref):
    rows, channels = att_ref.shape
    taps = table_ref.shape[1] // 2
    per_lane_tile = 128 * table_ref.shape[0] // (taps * channels)
    ones = jnp.ones((sq_ref.shape[0], 128), F32)
    summed = lax.dot_general(
        sq_ref[:, 0, :], ones, (((0,), (0,)), ((), ())),
        precision=HIGHEST, preferred_element_type=F32,
    )
    inverse = lax.rsqrt(summed / total_channels + EPS)
    for ref, at, size, start in ((halo_ref, 0, HALO, 0), (att_ref, HALO, rows, BLOCK)):
        for w in range(0, channels, 128):
            lanes = slice(w, w + 128)
            normed = (
                ref[:, lanes].astype(F32) * inverse[start : start + size] * coef_ref[9:10, lanes]
            ).astype(BF16)
            ext_ref[at : at + size, lanes] = normed.astype(F32)

    def branch(b, start, size, lanes=slice(None)):
        total = coef_ref[3 * b : 3 * b + 1, lanes] * ext_ref[start : start + size, lanes]
        for t in range(1, 3):
            total = total + coef_ref[3 * b + t : 3 * b + t + 1, lanes] * ext_ref[start - t : start - t + size, lanes]
        return total

    for r in range(0, rows + taps, taps):
        start = HALO - taps + r
        prod_ref[r : r + taps, :] = (branch(1, start, taps) * branch(2, start, taps)).astype(BF16)
    group = lax.broadcasted_iota(jnp.int32, (taps, 128), 1) // (128 // per_lane_tile)
    n = taps * per_lane_tile
    for w in range(0, channels, 128):
        lanes = slice(w, w + 128)
        at = (w // 128) * n
        for r in range(0, rows, 2 * taps):
            pair = jnp.concatenate(
                [prod_ref[r + d : r + d + 2 * taps, lanes] for d in (0, taps)], axis=1
            )
            mixed = jnp.dot(table_ref[at : at + n, :], pair, preferred_element_type=F32)
            for i in range(2):
                ri = r + i * taps
                long_mix = mixed[:taps, i * 128 : (i + 1) * 128]
                for g in range(1, per_lane_tile):
                    long_mix = jnp.where(
                        group == g, mixed[g * taps : (g + 1) * taps, i * 128 : (i + 1) * 128], long_mix
                    )
                query = branch(0, HALO + ri, taps, lanes)
                out_ref[ri : ri + taps, lanes] = (
                    att_ref[ri : ri + taps, lanes].astype(F32) + query * long_mix
                ).astype(BF16)


def array(*dims, dtype=BF16):
    return jax.ShapeDtypeStruct(dims, dtype)


def call(kernel, out_shape, args, scratch=(), flops=0, mib=8, spec=VMEM):
    outs = out_shape if isinstance(out_shape, tuple) else (out_shape,)
    nbytes = sum(math.prod(a.shape) * a.dtype.itemsize for a in (*args, *outs))
    result = pl.pallas_call(
        kernel,
        out_shape=outs,
        in_specs=[spec] * len(args),
        out_specs=tuple(VMEM for _ in outs),
        scratch_shapes=list(scratch),
        cost_estimate=pl.CostEstimate(flops=flops, bytes_accessed=nbytes, transcendentals=0),
        compiler_params=pltpu.CompilerParams(vmem_limit_bytes=mib << 20),
    )(*args)
    return result if isinstance(out_shape, tuple) else result[0]


def per_device(queries, keys, values, norm_gain, short_filters, medium_filters):
    rows, channels = queries.shape
    taps, groups = medium_filters.shape
    count = lax.axis_size("ctx")
    peers = lax.axis_size("fsdp")
    ahead = [(i, i + 2) for i in range(count - 2)]
    beside = [(i, i ^ 1) for i in range(count)]

    behind_three = [(i, i + 3) for i in range(1, count - 3, 2)]

    half = array(rows, channels)
    full = array(rows, channels, dtype=F32)
    k2 = lax.ppermute(keys, "ctx", ahead)
    vq = jnp.concatenate([values, queries[rows - HALO :]], axis=0)
    vq2 = lax.ppermute(vq, "ctx", ahead)
    tails = jnp.concatenate([keys[rows - BLOCK :], values[rows - BLOCK :]], axis=0)
    tails3 = lax.ppermute(tails, "ctx", behind_three)
    q, k = queries, keys
    picked = call(pick_keys_kernel, array(rows + BLOCK, channels), (k, k2))
    k1 = lax.ppermute(picked, "ctx", beside)
    peak, total, acc, table, coef = call(
        early_kernel,
        (full, full, full, array(groups * taps, 2 * taps), array(16, channels, dtype=F32)),
        (q, k, vq, medium_filters.T, short_filters, norm_gain.reshape(1, channels)),
        flops=300 << 20, mib=12,
    )
    picked = call(pick_values_kernel, array(rows + HALO + BLOCK, channels), (vq, vq2, peak))
    v1 = lax.ppermute(picked, "ctx", beside)
    peak, total, acc = call(
        far_kernel, (full, full, full), (q, k2, vq2, peak, total, acc),
        flops=300 << 20, mib=12,
    )
    attended, halo, squares = call(
        near_kernel, (half, array(HALO, channels), array(peers, 1, BLOCK + rows, dtype=F32)),
        (q, k2, vq2, k1, v1, tails3, peak, total, acc), flops=500 << 20, mib=16,
    )
    shared = lax.all_to_all(squares, "fsdp", 0, 0, tiled=True)
    return call(
        functools.partial(mix_kernel, channels * peers), half,
        (shared, halo, attended, coef, table),
        scratch=(
            pltpu.VMEM((rows + HALO, channels), F32),
            pltpu.VMEM((rows + taps, channels), BF16),
        ),
        flops=1 << 30, mib=12,
    )


def solution(mesh):
    placed = (
        P("ctx", "fsdp"),
        P("ctx", "fsdp"),
        P("ctx", "fsdp"),
        P("fsdp"),
        P(None, None, "fsdp"),
        P(None, "fsdp"),
    )

    return jax.shard_map(
        per_device, mesh=mesh, in_specs=placed, out_specs=P("ctx", "fsdp"), check_vma=False
    )
```

profile of v0, /device:TPU:768, one launch (start us, length us, event | category | flops | bytes accessed | tf_op | source)
XLA Modules:
  0.0 51.1 jit_solution(540202925333564273)
XLA Ops:
  0.0 0.9 %slice-done = bf16[144,256]{1,0:T(8,128)(2,1)S(1)} async-done(((bf16[512,256]{1,0:T(8,128)(2,1)}), bf16[144,256]{1,0:T(8,128)(2,1)S(1)}, s32[]{:S(2)}) %slice-start) | async-done | bytes 73752 | tf_op jit(solution)/shard_map/slice | solution.py:331
  0.9 1.0 %pad_maximum_fusion.v_ref.own_ref = bf16[656,256]{1,0:T(8,128)(2,1)S(1)} fusion(bf16[144,256]{1,0:T(8,128)(2,1)S(1)} %slice-done, bf16[512,256]{1,0:T(8,128)(2,1)} %param.8), kind=kLoop, calls=%fused_computation | loop fusion | flops 671744 | bytes 671744 | tf_op jit(solution)/shard_map/concatenate | solution.py:331
  1.9 4.9 %collective-permute-start.1 = (bf16[656,256]{1,0:T(8,128)(2,1)S(1)}, bf16[656,256]{1,0:T(8,128)(2,1)S(1)}, u32[]{:S(2)}, u32[]{:S(2)}) collective-permute-start(bf16[656,256]{1,0:T(8,128)(2,1)S(1)} %pad_maximum_fusion.v_ref.own_ref), channel_id=1, source_target_pairs={{0,16},{8,24},{16,32},{24,40},{32,48},{40,56},{48,64},{56,72},{64,... | collective-permute-start | bytes 1007624 | tf_op jit(solution)/shard_map/ppermute | solution.py:332
  6.9 0.0 copy-done.1
  6.9 2.9 %collective-permute-start = (bf16[512,256]{1,0:T(8,128)(2,1)S(1)}, bf16[512,256]{1,0:T(8,128)(2,1)S(1)}, u32[]{:S(2)}, u32[]{:S(2)}) collective-permute-start(bf16[512,256]{1,0:T(8,128)(2,1)S(1)} %copy-done.1), channel_id=1, source_target_pairs={{0,16},{8,24},{16,32},{24,40},{32,48},{40,56},{48,64},{56,72},{64,... | collective-permute-start | bytes 786440 | tf_op jit(solution)/shard_map/ppermute | solution.py:330
  9.8 0.0 copy-start.4
  9.8 0.0 copy-done
  9.8 0.0 copy-done.2
  9.8 0.6 %copy-done.4 = f32[256]{0:T(256)S(1)} copy-done((f32[256]{0:T(256)S(1)}, f32[256]{0:T(256)}, u32[]{:S(2)}) %copy-start.4) | copy-done | bytes 1048
  10.4 1.2 %shard_map.65 = (f32[512,256]{1,0:T(8,128)S(1)}, f32[512,256]{1,0:T(8,128)S(1)}, f32[512,256]{1,0:T(8,128)S(1)}, bf16[2048,256]{1,0:T(8,128)(2,1)S(1)}, f32[16,256]{1,0:T(8,128)S(1)}) custom-call(bf16[512,256]{1,0:T(8,128)(2,1)S(1)} %copy-done, bf16[512,256]{1,0:T(8,128)(2,1)S(1)} %copy-done.1, bf16[656,256]{1,0:T(8,128)(2,1)S(1)} %pad_maximum_fusion.v_ref.own_ref, ...), custom_call_target="tpu_custom_call" | custom-call | flops 314572800 | bytes 3512320 | tf_op jit(solution)/shard_map/pallas_call | solution.py:306
  11.6 6.6 %collective-permute-done.1.far_ref.v_ref.v2_ref = bf16[656,256]{1,0:T(8,128)(2,1)S(1)} collective-permute-done((bf16[656,256]{1,0:T(8,128)(2,1)S(1)}, bf16[656,256]{1,0:T(8,128)(2,1)S(1)}, u32[]{:S(2)}, u32[]{:S(2)}) %collective-permute-start.1) | collective-permute-done | bytes 335904 | tf_op jit(solution)/shard_map/ppermute | solution.py:332
  18.2 1.9 %collective-permute-start.3 = (bf16[912,256]{1,0:T(8,128)(2,1)S(1)}, bf16[912,256]{1,0:T(8,128)(2,1)S(1)}, u32[]{:S(2)}, u32[]{:S(2)}) collective-permute-start(bf16[912,256]{1,0:T(8,128)(2,1)S(1)} %shard_map.66), channel_id=1, source_target_pairs={{0,8},{8,0},{16,24},{24,16},{32,40},{40,32},{48,56},{56,48},{64,72... | collective-permute-start | bytes 1400840 | tf_op jit(solution)/shard_map/ppermute | solution.py:345
  20.2 2.5 %collective-permute-done.far_ref.k_ref.k2_ref = bf16[512,256]{1,0:T(8,128)(2,1)S(1)} collective-permute-done((bf16[512,256]{1,0:T(8,128)(2,1)S(1)}, bf16[512,256]{1,0:T(8,128)(2,1)S(1)}, u32[]{:S(2)}, u32[]{:S(2)}) %collective-permute-start) | collective-permute-done | bytes 262176 | tf_op jit(solution)/shard_map/ppermute | solution.py:330
  22.7 1.9 %collective-permute-start.2 = (bf16[768,256]{1,0:T(8,128)(2,1)S(1)}, bf16[768,256]{1,0:T(8,128)(2,1)S(1)}, u32[]{:S(2)}, u32[]{:S(2)}) collective-permute-start(bf16[768,256]{1,0:T(8,128)(2,1)S(1)} %shard_map.64), channel_id=1, source_target_pairs={{0,8},{8,0},{16,24},{24,16},{32,40},{40,32},{48,56},{56,48},{64,72... | collective-permute-start | bytes 1179656 | tf_op jit(solution)/shard_map/ppermute | solution.py:337
  24.7 0.0 slice-start.1
  24.7 0.9 %slice-done.1 = bf16[256,256]{1,0:T(8,128)(2,1)S(1)} async-done(((bf16[512,256]{1,0:T(8,128)(2,1)}), bf16[256,256]{1,0:T(8,128)(2,1)S(1)}, s32[]{:S(2)}) %slice-start.1) | async-done | bytes 131096 | tf_op jit(solution)/shard_map/slice | solution.py:333
  25.6 1.3 %collective-permute-start.4 = (bf16[512,256]{1,0:T(8,128)(2,1)S(1)}, bf16[512,256]{1,0:T(8,128)(2,1)S(1)}, u32[]{:S(2)}, u32[]{:S(2)}) collective-permute-start(bf16[512,256]{1,0:T(8,128)(2,1)S(1)} %pad_maximum_fusion.1), channel_id=1, source_target_pairs={{8,32},{24,48},{40,64},{56,80},{72,96},{88,112},{104,128},{120,144... | collective-permute-start | bytes 786440 | tf_op jit(solution)/shard_map/ppermute | solution.py:334
  26.9 1.0 %shard_map.67 = (f32[512,256]{1,0:T(8,128)S(1)}, f32[512,256]{1,0:T(8,128)S(1)}, f32[512,256]{1,0:T(8,128)S(1)}) custom-call(bf16[512,256]{1,0:T(8,128)(2,1)S(1)} %copy-done, bf16[512,256]{1,0:T(8,128)(2,1)S(1)} %collective-permute-done.far_ref.k_ref.k2_ref, bf16[656,256]{1,0:T(8,128)(2,1)S(1)} %collective-permute-done.1.far_ref.v_ref.v2_ref, ...), custom_call_target="tpu_custom_call" | custom-call | flops 314572800 | bytes 4005888 | tf_op jit(solution)/shard_map/pallas_call | solution.py:306
  27.9 6.6 %collective-permute-done.4.tails_ref = bf16[512,256]{1,0:T(8,128)(2,1)S(1)} collective-permute-done((bf16[512,256]{1,0:T(8,128)(2,1)S(1)}, bf16[512,256]{1,0:T(8,128)(2,1)S(1)}, u32[]{:S(2)}, u32[]{:S(2)}) %collective-permute-start.4) | collective-permute-done | bytes 262176 | tf_op jit(solution)/shard_map/ppermute | solution.py:334
  34.5 0.0 collective-permute-done.2.k1_ref
  34.5 0.0 collective-permute-done.3.v1_ref
  34.5 2.3 %shard_map.68 = (bf16[512,256]{1,0:T(8,128)(2,1)S(1)}, bf16[144,256]{1,0:T(8,128)(2,1)S(1)}, f32[8,1,768]{2,1,0:T(1,128)S(1)}) custom-call(bf16[512,256]{1,0:T(8,128)(2,1)S(1)} %copy-done, bf16[512,256]{1,0:T(8,128)(2,1)S(1)} %collective-permute-done.far_ref.k_ref.k2_ref, bf16[656,256]{1,0:T(8,128)(2,1)S(1)} %collective-permute-done.1.far_ref.v_ref.v2_ref, ...), custom_call_target="tpu_custom_call" | custom-call | flops 524288000 | bytes 3915776 | tf_op jit(solution)/shard_map/pallas_call | solution.py:306
  36.8 11.4 %all_to_all.5.sq_ref = f32[8,1,768]{2,1,0:T(1,128)S(1)} all-to-all(f32[8,1,768]{2,1,0:T(1,128)S(1)} %get-tuple-element.22), channel_id=1, replica_groups=mesh['ctx'=128,'fsdp'=8] {'fsdp'}, dimensions={0} | all-to-all | bytes 49152 | tf_op jit(solution)/shard_map/all_to_all | solution.py:354
  48.2 2.9 %shard_map.69 = bf16[512,256]{1,0:T(8,128)(2,1)} custom-call(f32[8,1,768]{2,1,0:T(1,128)S(1)} %all_to_all.5.sq_ref, bf16[144,256]{1,0:T(8,128)(2,1)S(1)} %get-tuple-element.23.halo_ref, bf16[512,256]{1,0:T(8,128)(2,1)S(1)} %get-tuple-element.24.att_ref, f32[16,256]{1,0:T(8,128)S(1)} %get-tuple-element.25.coef_ref, ...), custom_call_target="tpu_custom_call" | custom-call | flops 1073741824 | bytes 1687552 | tf_op jit(solution)/shard_map/pallas_call | solution.py:306
  (10 shorter events, 0.1 us)
Async XLA Ops:
  0.0 0.9 %slice-start = ((bf16[512,256]{1,0:T(8,128)(2,1)}), bf16[144,256]{1,0:T(8,128)(2,1)S(1)}, s32[]{:S(2)}) async-start(bf16[512,256]{1,0:T(8,128)(2,1)} %q_ref.5), calls=%async_computation.1 | async-start | bytes 147456 | tf_op jit(solution)/shard_map/slice | solution.py:331
  0.9 6.0 %copy-start.1 = (bf16[512,256]{1,0:T(8,128)(2,1)S(1)}, bf16[512,256]{1,0:T(8,128)(2,1)}, u32[]{:S(2)}) copy-start(bf16[512,256]{1,0:T(8,128)(2,1)} %k_ref.1) | copy-start | bytes 786436
  0.9 8.9 %copy-start = (bf16[512,256]{1,0:T(8,128)(2,1)S(1)}, bf16[512,256]{1,0:T(8,128)(2,1)}, u32[]{:S(2)}) copy-start(bf16[512,256]{1,0:T(8,128)(2,1)} %q_ref.5) | copy-start | bytes 786436
  0.9 8.9 %copy-start.2 = (f32[3,3,256]{2,1,0:T(4,128)S(1)}, f32[3,3,256]{2,1,0:T(4,128)}, u32[]{:S(2)}) copy-start(f32[3,3,256]{2,1,0:T(4,128)} %short_ref.1) | copy-start | bytes 27652
  0.9 8.9 %copy-start.3 = (bf16[128,16]{0,1:T(8,128)(2,1)S(1)}, bf16[128,16]{0,1:T(8,128)(2,1)}, u32[]{:S(2)}) copy-start(bf16[128,16]{0,1:T(8,128)(2,1)} %param.11) | copy-start | bytes 12292
  1.9 16.3 %collective-permute-start.1 = (bf16[656,256]{1,0:T(8,128)(2,1)S(1)}, bf16[656,256]{1,0:T(8,128)(2,1)S(1)}, u32[]{:S(2)}, u32[]{:S(2)}) collective-permute-start(bf16[656,256]{1,0:T(8,128)(2,1)S(1)} %pad_maximum_fusion.v_ref.own_ref), channel_id=1, source_target_pairs={{0,16},{8,24},{16,32},{24,40},{32,48},{40,56},{48,64},{56,72},{64,... | collective-permute-start | bytes 1007624 | tf_op jit(solution)/shard_map/ppermute | solution.py:332
  6.9 15.8 %collective-permute-start = (bf16[512,256]{1,0:T(8,128)(2,1)S(1)}, bf16[512,256]{1,0:T(8,128)(2,1)S(1)}, u32[]{:S(2)}, u32[]{:S(2)}) collective-permute-start(bf16[512,256]{1,0:T(8,128)(2,1)S(1)} %copy-done.1), channel_id=1, source_target_pairs={{0,16},{8,24},{16,32},{24,40},{32,48},{40,56},{48,64},{56,72},{64,... | collective-permute-start | bytes 786440 | tf_op jit(solution)/shard_map/ppermute | solution.py:330
  9.8 0.7 %copy-start.4 = (f32[256]{0:T(256)S(1)}, f32[256]{0:T(256)}, u32[]{:S(2)}) copy-start(f32[256]{0:T(256)} %param.9) | copy-start | bytes 3076
  18.2 16.3 %collective-permute-start.3 = (bf16[912,256]{1,0:T(8,128)(2,1)S(1)}, bf16[912,256]{1,0:T(8,128)(2,1)S(1)}, u32[]{:S(2)}, u32[]{:S(2)}) collective-permute-start(bf16[912,256]{1,0:T(8,128)(2,1)S(1)} %shard_map.66), channel_id=1, source_target_pairs={{0,8},{8,0},{16,24},{24,16},{32,40},{40,32},{48,56},{56,48},{64,72... | collective-permute-start | bytes 1400840 | tf_op jit(solution)/shard_map/ppermute | solution.py:345
  22.7 11.8 %collective-permute-start.2 = (bf16[768,256]{1,0:T(8,128)(2,1)S(1)}, bf16[768,256]{1,0:T(8,128)(2,1)S(1)}, u32[]{:S(2)}, u32[]{:S(2)}) collective-permute-start(bf16[768,256]{1,0:T(8,128)(2,1)S(1)} %shard_map.64), channel_id=1, source_target_pairs={{0,8},{8,0},{16,24},{24,16},{32,40},{40,32},{48,56},{56,48},{64,72... | collective-permute-start | bytes 1179656 | tf_op jit(solution)/shard_map/ppermute | solution.py:337
  24.7 0.9 %slice-start.1 = ((bf16[512,256]{1,0:T(8,128)(2,1)}), bf16[256,256]{1,0:T(8,128)(2,1)S(1)}, s32[]{:S(2)}) async-start(bf16[512,256]{1,0:T(8,128)(2,1)} %param.8), calls=%async_computation.2 | async-start | bytes 262144 | tf_op jit(solution)/shard_map/slice | solution.py:333
  25.6 8.9 %collective-permute-start.4 = (bf16[512,256]{1,0:T(8,128)(2,1)S(1)}, bf16[512,256]{1,0:T(8,128)(2,1)S(1)}, u32[]{:S(2)}, u32[]{:S(2)}) collective-permute-start(bf16[512,256]{1,0:T(8,128)(2,1)S(1)} %pad_maximum_fusion.1), channel_id=1, source_target_pairs={{8,32},{24,48},{40,64},{56,80},{72,96},{88,112},{104,128},{120,144... | collective-permute-start | bytes 786440 | tf_op jit(solution)/shard_map/ppermute | solution.py:334
where the time goes:
time: 51.4 us; the launch traced here: 51.1 us
  waiting for transfers between devices  15.7 us (31%)
  starting transfers between devices  12.9 us (25%)
  blocking collectives  11.4 us (22%)
  Pallas kernels  7.36 us (14%)
  local copies, waits for them, and re-layouts  2.45 us (5%)
  other arithmetic  1.05 us (2%)
    all_to_all x1, blocking collectives, per_device(): shared = lax.all_to_all(squares, 'fsdp', 0, 0, tiled=True)  11.4 us
    pallas_call x6, Pallas kernels, call(): pl.pallas_call(kernel, out_shape=outs, in_specs=[spec] * len(args), out_s...  7.36 us
    ppermute x1, waiting for transfers between devices, per_device(): tails3 = lax.ppermute(tails, 'ctx', behind_three)  6.64 us
    ppermute x1, waiting for transfers between devices, per_device(): vq2 = lax.ppermute(vq, 'ctx', ahead)  6.58 us
    ppermute x1, starting transfers between devices, per_device(): vq2 = lax.ppermute(vq, 'ctx', ahead)  4.93 us
    ppermute x1, starting transfers between devices, per_device(): k2 = lax.ppermute(keys, 'ctx', ahead)  2.87 us
    ppermute x1, waiting for transfers between devices, per_device(): k2 = lax.ppermute(keys, 'ctx', ahead)  2.52 us
    ppermute x1, starting transfers between devices, per_device(): v1 = lax.ppermute(picked, 'ctx', beside)  1.92 us
  transfers between devices with their start and end apart: 5, of which 3 were waited for; matrix products, arithmetic and copies ran while one was open for 0% of the time, Pallas kernels for 4%

commit v1 on v0

v1 whole, which is shorter than its diff:
```python
import functools
import math

import jax
import jax.numpy as jnp
from jax import lax
from jax.experimental import pallas as pl
from jax.experimental.pallas import tpu as pltpu
from jax.sharding import PartitionSpec as P


HEAD_DIM = 128
BLOCK = 256
HALO = 144
TAIL = 128
NEG = -1e30
EPS = 1e-6
LOG2E = 1.4426950408889634
SCALE = LOG2E / math.sqrt(HEAD_DIM)
VMEM = pl.BlockSpec(memory_space=pltpu.VMEM)
HBM = pl.BlockSpec(memory_space=pltpu.HBM)
F32 = jnp.float32
BF16 = jnp.bfloat16


def cols_of(h):
    return slice(h * HEAD_DIM, (h + 1) * HEAD_DIM)


def peak_of(unit):
    q, groups, state = unit
    rows = q.shape[0]
    scores = []
    peak = None
    for pieces, gone in groups:
        top = None
        for k, v, mask in pieces:
            s = lax.dot_general(q, k, (((1,), (1,)), ((), ())), preferred_element_type=F32)
            if mask is not None:
                s = jnp.where(mask, s, NEG)
            scores.append((s, v, gone))
            for w in range(0, s.shape[1], 128):
                piece = s[:, w : w + 128]
                top = piece if top is None else jnp.maximum(top, piece)
        if gone is not None:
            top = top - gone
        peak = top if peak is None else jnp.maximum(peak, top)
    peak = jnp.broadcast_to(jnp.max(peak, axis=1, keepdims=True), (rows, 128))
    if state is not None:
        peak = jnp.maximum(state[0], peak)
    return scores, peak


def weigh(unit, scores, peak):
    total = acc = None
    if unit[2] is not None:
        before, total, acc = unit[2]
        shrink = jnp.exp2((before - peak) * SCALE)
        total, acc = total * shrink, acc * shrink
    for s, v, gone in scores:
        off = peak if gone is None else peak + gone
        halves = []
        for w in range(0, s.shape[1], 128):
            p = jnp.exp2((s[:, w : w + 128] - off) * SCALE)
            total = p if total is None else total + p
            halves.append(p.astype(BF16))
        o = jnp.dot(jnp.concatenate(halves, axis=1) if len(halves) > 1 else halves[0], v, preferred_element_type=F32)
        acc = o if acc is None else acc + o
    return peak, total, acc


def exponents(unit, scores, peak):
    shrink = total = None
    if unit[2] is not None:
        shrink = jnp.exp2((unit[2][0] - peak) * SCALE)
        total = unit[2][1] * shrink
    pieces = []
    for s, _, gone in scores:
        off = peak if gone is None else peak + gone
        for w in range(0, s.shape[1], 128):
            p = jnp.exp2((s[:, w : w + 128] - off) * SCALE)
            total = p if total is None else total + p
            pieces.append(p.astype(BF16))
    inverse = 1.0 / jnp.sum(total, axis=1, keepdims=True)
    return shrink, jnp.broadcast_to(inverse, total.shape), pieces


def run_units(units, then, done):
    ahead = peak_of(units[0][0])
    for i, (unit, tag) in enumerate(units):
        now = ahead
        if i + 1 < len(units):
            ahead = peak_of(units[i + 1][0])
        done(tag, then(unit, *now))


def finish(state):
    _, total, acc = state
    return (acc / jnp.sum(total, axis=1, keepdims=True)).astype(BF16)


def part(i):
    return slice(i * BLOCK, (i + 1) * BLOCK)


def grid_iota():
    shape = (BLOCK, BLOCK)
    return lax.broadcasted_iota(jnp.int32, shape, 0), lax.broadcasted_iota(jnp.int32, shape, 1)


def absent(distance):
    return jnp.where(lax.axis_index("ctx") >= distance, 0.0, -NEG).astype(F32)


def is_even():
    return lax.rem(lax.axis_index("ctx"), 2) == 0


def early_kernel(
    q_ref, k_ref, v_ref, peak_ref, total_ref, acc_ref,
):
    rows, channels = q_ref.shape
    ri, ci = grid_iota()
    units = []
    for h in range(channels // HEAD_DIM):
        cols = cols_of(h)
        for b in range(rows // BLOCK):
            pieces = [
                (k_ref[part(j), cols], v_ref[part(j), cols], ci <= ri if j == b else None)
                for j in range(b + 1)
            ]
            units.append(((q_ref[part(b), cols], [(pieces, None)], None), (part(b), cols)))

    def done(tag, state):
        peak_ref[tag], total_ref[tag], acc_ref[tag] = state

    run_units(units, weigh, done)


def pick_kernel(rows, own_ref, far_ref, *refs):
    out_ref = refs[-1]
    size = own_ref.shape[0]

    @pl.when(is_even())
    def _():
        out_ref[:size, :] = own_ref[...]
        out_ref[size:, :] = far_ref[rows - TAIL : rows, :]

    @pl.when(jnp.logical_not(is_even()))
    def _():
        out_ref[:size, :] = far_ref[...]


def score_kernel(
    q_ref, k2_ref, k1_ref, peak_in, total_in, near_ref, far_ref, shrink_ref, inv_ref
):
    rows, channels = q_ref.shape
    heads = channels // HEAD_DIM
    blocks = rows // BLOCK
    ri, ci = grid_iota()
    units = []
    for b in range(blocks):
        for h in range(heads):
            cols = cols_of(h)
            tag = (part(b), cols)
            near = [(k1_ref[part(j), cols], None, None) for j in range(blocks)]
            far = [
                (k2_ref[part(j), cols], None, ci > ri if j == b else None)
                for j in range(b, blocks)
            ]
            state = (peak_in[tag], total_in[tag], None)
            units.append(((q_ref[tag], [(near, absent(1)), (far, absent(2))], state), (b, h)))

    def done(tag, result):
        b, h = tag
        shrink, inverse, pieces = result
        shrink_ref[part(b), cols_of(h)] = shrink
        inv_ref[part(b), cols_of(h)] = inverse
        for i, p in enumerate(pieces):
            key = i * 128
            ref = near_ref
            if key >= rows:
                ref, key = far_ref, key - rows + b * BLOCK
            ref[part(b), h * rows + key : h * rows + key + 128] = p

    run_units(units, exponents, done)


def far_values_kernel(
    far_ref, shrink_ref, acc_ref, v2_ref, filt_ref, short_ref, gain_ref, out_ref, table_ref, coef_ref
):
    rows, channels = acc_ref.shape
    for h in range(channels // HEAD_DIM):
        cols = cols_of(h)
        for b in range(rows // BLOCK):
            keys = slice(h * rows + b * BLOCK, (h + 1) * rows)
            out_ref[part(b), cols] = acc_ref[part(b), cols] * shrink_ref[part(b), cols] + jnp.dot(
                far_ref[part(b), keys], v2_ref[b * BLOCK : rows, cols], preferred_element_type=F32
            )
    groups, taps = filt_ref.shape
    tap = lax.broadcasted_iota(jnp.int32, (taps, 2 * taps), 0)
    ext = lax.broadcasted_iota(jnp.int32, (taps, 2 * taps), 1)
    flip = jnp.where(ext == taps - tap, 1.0, 0.0).astype(BF16)
    base = jnp.dot(filt_ref[...], flip, preferred_element_type=F32)
    for g in range(groups):
        row = jnp.broadcast_to(base[g : g + 1, :], (taps, 2 * taps))
        shifted = pltpu.roll(row, 0, 1, stride=1, stride_axis=0)
        table_ref[g * taps : (g + 1) * taps, :] = shifted.astype(BF16)
    for i in range(9):
        coef_ref[i : i + 1, :] = short_ref[i // 3, i % 3 : i % 3 + 1, :]
    coef_ref[9:10, :] = gain_ref[...]


def row_squares(att):
    af = att.astype(F32)
    af = af * af
    high = af.astype(BF16)
    low = (af - high.astype(F32)).astype(BF16)
    ones = jnp.ones((8, af.shape[1]), BF16)
    dims = (((1,), (1,)), ((), ()))
    return lax.dot_general(ones, high, dims, preferred_element_type=F32) + lax.dot_general(
        ones, low, dims, preferred_element_type=F32
    )


def values_kernel(
    near_ref, inv_ref, acc_ref, k2_ref, v2_ref, k1_ref, v1_ref, tails_ref, out_ref, halo_out, sq_ref
):
    rows, channels = out_ref.shape
    heads = channels // HEAD_DIM
    blocks = rows // BLOCK
    shift = BLOCK - HALO
    sq_ref[:, 0, :BLOCK] = jnp.zeros((sq_ref.shape[0], BLOCK), F32)
    hr = lax.broadcasted_iota(jnp.int32, (HALO, BLOCK), 0)
    hc = lax.broadcasted_iota(jnp.int32, (HALO, BLOCK), 1)
    tr = lax.broadcasted_iota(jnp.int32, (HALO, TAIL), 0)
    tc = lax.broadcasted_iota(jnp.int32, (HALO, TAIL), 1)
    units = []
    for h in range(heads):
        cols = cols_of(h)
        q = v1_ref[rows : rows + HALO, cols]
        k3 = jnp.where(is_even(), tails_ref[:TAIL, cols], k1_ref[rows:, cols])
        v3 = jnp.where(is_even(), tails_ref[TAIL:, cols], v1_ref[rows + HALO :, cols])
        near = [(k1_ref[part(j), cols], v1_ref[part(j), cols], None) for j in range(blocks)]
        near[-1] = (*near[-1][:2], hc <= hr + shift)
        middle = [(k2_ref[part(j), cols], v2_ref[part(j), cols], None) for j in range(blocks)]
        groups = [
            (near, absent(1)),
            (middle, absent(2)),
            ([(k3, v3, tc > tr + TAIL - HALO)], absent(3)),
        ]
        units.append((q, groups, None))

    def main(b):
        for h in range(heads):
            cols = cols_of(h)
            total = acc_ref[part(b), cols] + jnp.dot(
                near_ref[part(b), h * rows : (h + 1) * rows], v1_ref[:rows, cols],
                preferred_element_type=F32,
            )
            out_ref[part(b), cols] = (total * inv_ref[part(b), cols]).astype(BF16)
        sq_ref[:, 0, part(b + 1)] = row_squares(out_ref[part(b), :])

    ahead = [peak_of(unit) for unit in units]
    for i in range(max(heads, blocks)):
        if i < blocks:
            main(i)
        if i < heads:
            att = finish(weigh(units[i], *ahead[i]))
            halo_out[:, cols_of(i)] = jnp.where(
                lax.axis_index("ctx") >= 1, att, jnp.zeros(att.shape, BF16)
            )
    sq_ref[:, 0, :HALO] = row_squares(halo_out[...])


def mix_kernel(
    total_channels, sq_ref, halo_ref, att_ref, coef_ref, table_ref, out_ref, ext_ref, prod_ref, query_ref
):
    rows, channels = att_ref.shape
    taps = table_ref.shape[1] // 2
    per_lane_tile = 128 * table_ref.shape[0] // (taps * channels)
    summed = jnp.sum(sq_ref[:, 0, :], axis=0, keepdims=True)
    inverse = jnp.broadcast_to(lax.rsqrt(summed / total_channels + EPS), (8, summed.shape[1]))
    high = inverse.astype(BF16)
    rest = inverse - high.astype(F32)
    middle = rest.astype(BF16)
    low = (rest - middle.astype(F32)).astype(BF16)
    first = lax.broadcasted_iota(jnp.int32, (8, 128), 0) == 0
    ones = jnp.where(first, 1.0, 0.0).astype(BF16)
    dims = (((0,), (0,)), ((), ()))
    columns = (
        lax.dot_general(high, ones, dims, preferred_element_type=F32)
        + lax.dot_general(middle, ones, dims, preferred_element_type=F32)
    ) + lax.dot_general(low, ones, dims, preferred_element_type=F32)
    for ref, at, size, start in ((halo_ref, 0, HALO, 0), (att_ref, HALO, rows, BLOCK)):
        for w in range(0, channels, 128):
            lanes = slice(w, w + 128)
            normed = (
                ref[:, lanes].astype(F32) * columns[start : start + size] * coef_ref[9:10, lanes]
            ).astype(BF16)
            ext_ref[at : at + size, lanes] = normed.astype(F32)

    for w in range(0, channels, 128):
        lanes = slice(w, w + 128)
        for r in range(0, rows + taps, taps):
            start = HALO - taps + r
            shifted = [ext_ref[start - t : start - t + taps, lanes] for t in range(3)]
            branch = []
            for b in range(3):
                total = coef_ref[3 * b : 3 * b + 1, lanes] * shifted[0]
                for t in range(1, 3):
                    total = total + coef_ref[3 * b + t : 3 * b + t + 1, lanes] * shifted[t]
                branch.append(total)
            prod_ref[r : r + taps, lanes] = (branch[1] * branch[2]).astype(BF16)
            if r >= taps:
                query_ref[r - taps : r, lanes] = branch[0]
    group = lax.broadcasted_iota(jnp.int32, (taps, 128), 1) // (128 // per_lane_tile)
    n = taps * per_lane_tile
    for w in range(0, channels, 128):
        lanes = slice(w, w + 128)
        at = (w // 128) * n
        for r in range(0, rows, 2 * taps):
            pair = jnp.concatenate(
                [prod_ref[r + d : r + d + 2 * taps, lanes] for d in (0, taps)], axis=1
            )
            mixed = jnp.dot(table_ref[at : at + n, :], pair, preferred_element_type=F32)
            for i in range(2):
                ri = r + i * taps
                long_mix = mixed[:taps, i * 128 : (i + 1) * 128]
                for g in range(1, per_lane_tile):
                    long_mix = jnp.where(
                        group == g, mixed[g * taps : (g + 1) * taps, i * 128 : (i + 1) * 128], long_mix
                    )
                out_ref[ri : ri + taps, lanes] = (
                    att_ref[ri : ri + taps, lanes].astype(F32) + query_ref[ri : ri + taps, lanes] * long_mix
                ).astype(BF16)


def array(*dims, dtype=BF16):
    return jax.ShapeDtypeStruct(dims, dtype)


def call(kernel, out_shape, args, scratch=(), flops=0, mib=8, spec=VMEM):
    outs = out_shape if isinstance(out_shape, tuple) else (out_shape,)
    nbytes = sum(math.prod(a.shape) * a.dtype.itemsize for a in (*args, *outs))
    result = pl.pallas_call(
        kernel,
        out_shape=outs,
        in_specs=[spec] * len(args),
        out_specs=tuple(VMEM for _ in outs),
        scratch_shapes=list(scratch),
        cost_estimate=pl.CostEstimate(flops=flops, bytes_accessed=nbytes, transcendentals=0),
        compiler_params=pltpu.CompilerParams(vmem_limit_bytes=mib << 20),
    )(*args)
    return result if isinstance(out_shape, tuple) else result[0]


def per_device(queries, keys, values, norm_gain, short_filters, medium_filters):
    rows, channels = queries.shape
    taps, groups = medium_filters.shape
    count = lax.axis_size("ctx")
    peers = lax.axis_size("fsdp")
    heads = channels // HEAD_DIM
    ahead = [(i, i + 2) for i in range(count - 2)]
    beside = [(i, i ^ 1) for i in range(count)]

    behind_three = [(i, i + 3) for i in range(1, count - 3, 2)]

    half = array(rows, channels)
    full = array(rows, channels, dtype=F32)
    k2 = lax.ppermute(keys, "ctx", ahead)
    vq = jnp.concatenate([values, queries[rows - HALO :]], axis=0)
    vq2 = lax.ppermute(vq, "ctx", ahead)
    tails = jnp.concatenate([keys[rows - TAIL :], values[rows - TAIL :]], axis=0)
    tails3 = lax.ppermute(tails, "ctx", behind_three)
    pick = functools.partial(pick_kernel, rows)
    picked = call(pick, array(rows + TAIL, channels), (keys, k2))
    k1 = lax.ppermute(picked, "ctx", beside)
    peak, total, acc = call(
        early_kernel, (full, full, full), (queries, keys, vq), flops=300 << 20, mib=12
    )
    wide = array(rows, heads * rows)
    p_near, p_far, shrink, inverse = call(
        score_kernel, (wide, wide, full, full), (queries, k2, k1, peak, total),
        flops=400 << 20, mib=16,
    )
    picked = call(pick, array(rows + HALO + TAIL, channels), (vq, vq2))
    v1 = lax.ppermute(picked, "ctx", beside)
    acc, table, coef = call(
        far_values_kernel,
        (full, array(groups * taps, 2 * taps), array(16, channels, dtype=F32)),
        (
            p_far, shrink, acc, vq2,
            medium_filters.T, short_filters, norm_gain.reshape(1, channels),
        ),
        flops=200 << 20, mib=12,
    )
    attended, halo, squares = call(
        values_kernel, (half, array(HALO, channels), array(peers, 1, BLOCK + rows, dtype=F32)),
        (p_near, inverse, acc, k2, vq2, k1, v1, tails3), flops=500 << 20, mib=16,
    )
    shared = lax.all_to_all(squares, "fsdp", 0, 0, tiled=True)
    return call(
        functools.partial(mix_kernel, channels * peers), half,
        (shared, halo, attended, coef, table),
        scratch=(
            pltpu.VMEM((rows + HALO, channels), F32),
            pltpu.VMEM((rows + taps, channels), BF16),
            pltpu.VMEM((rows, channels), F32),
        ),
        flops=1 << 30, mib=12,
    )


def solution(mesh):
    placed = (
        P("ctx", "fsdp"),
        P("ctx", "fsdp"),
        P("ctx", "fsdp"),
        P("fsdp"),
        P(None, None, "fsdp"),
        P(None, "fsdp"),
    )

    return jax.shard_map(
        per_device, mesh=mesh, in_specs=placed, out_specs=P("ctx", "fsdp"), check_vma=False
    )
```

time: 51.4 us -> 48.1 us (0.936)
  the two profiles are of different devices: /device:TPU:768 before, /device:TPU:353 now
where the time goes in v1:
time: 48.1 us; the launch traced here: 47.8 us
  starting transfers between devices  23.4 us (49%)
  blocking collectives  10 us (21%)
  Pallas kernels  6.93 us (14%)
  waiting for transfers between devices  4.7 us (10%)
  local copies, waits for them, and re-layouts  1.58 us (3%)
  other arithmetic  1.03 us (2%)
    all_to_all x1, blocking collectives, per_device(): shared = lax.all_to_all(squares, 'fsdp', 0, 0, tiled=True)  10 us
    pallas_call x7, Pallas kernels, call(): pl.pallas_call(kernel, out_shape=outs, in_specs=[spec] * len(args), out_s...  6.93 us
    ppermute x1, starting transfers between devices, per_device(): tails3 = lax.ppermute(tails, 'ctx', behind_three)  5.87 us
    ppermute x1, starting transfers between devices, per_device(): k2 = lax.ppermute(keys, 'ctx', ahead)  4.7 us
    ppermute x1, starting transfers between devices, per_device(): vq2 = lax.ppermute(vq, 'ctx', ahead)  4.65 us
    ppermute x1, starting transfers between devices, per_device(): v1 = lax.ppermute(picked, 'ctx', beside)  4.58 us
    ppermute x1, waiting for transfers between devices, per_device(): vq2 = lax.ppermute(vq, 'ctx', ahead)  3.69 us
    ppermute x1, starting transfers between devices, per_device(): k1 = lax.ppermute(picked, 'ctx', beside)  3.58 us
  transfers between devices with their start and end apart: 5, of which 2 were waited for; matrix products, arithmetic and copies ran while one was open for 0% of the time, Pallas kernels for 6%

profile of v1, /device:TPU:353, one launch (start us, length us, event | category | flops | bytes accessed | tf_op | source)
XLA Modules:
  0.0 47.8 jit_solution(4545984203895692007)
XLA Ops:
  0.0 0.9 %slice-done = bf16[144,256]{1,0:T(8,128)(2,1)S(1)} async-done(((bf16[512,256]{1,0:T(8,128)(2,1)}), bf16[144,256]{1,0:T(8,128)(2,1)S(1)}, s32[]{:S(2)}) %slice-start) | async-done | bytes 73752 | tf_op jit(solution)/shard_map/slice | solution.py:372
  0.9 1.0 %pad_maximum_fusion.v_ref.own_ref = bf16[656,256]{1,0:T(8,128)(2,1)S(1)} fusion(bf16[144,256]{1,0:T(8,128)(2,1)S(1)} %slice-done, bf16[512,256]{1,0:T(8,128)(2,1)} %param.8), kind=kLoop, calls=%fused_computation | loop fusion | flops 671744 | bytes 671744 | tf_op jit(solution)/shard_map/concatenate | solution.py:372
  1.9 4.7 %collective-permute-start.2 = (bf16[656,256]{1,0:T(8,128)(2,1)S(1)}, bf16[656,256]{1,0:T(8,128)(2,1)S(1)}, u32[]{:S(2)}, u32[]{:S(2)}) collective-permute-start(bf16[656,256]{1,0:T(8,128)(2,1)S(1)} %pad_maximum_fusion.v_ref.own_ref), channel_id=1, source_target_pairs={{0,16},{8,24},{16,32},{24,40},{32,48},{40,56},{48,64},{56,72},{64,... | collective-permute-start | bytes 1007624 | tf_op jit(solution)/shard_map/ppermute | solution.py:373
  6.6 4.7 %collective-permute-start = (bf16[512,256]{1,0:T(8,128)(2,1)S(1)}, bf16[512,256]{1,0:T(8,128)(2,1)S(1)}, u32[]{:S(2)}, u32[]{:S(2)}) collective-permute-start(bf16[512,256]{1,0:T(8,128)(2,1)S(1)} %copy-done.1), channel_id=1, source_target_pairs={{0,16},{8,24},{16,32},{24,40},{32,48},{40,56},{48,64},{56,72},{64,... | collective-permute-start | bytes 786440 | tf_op jit(solution)/shard_map/ppermute | solution.py:371
  11.3 3.7 %collective-permute-done.2.v2_ref.far_ref = bf16[656,256]{1,0:T(8,128)(2,1)S(1)} collective-permute-done((bf16[656,256]{1,0:T(8,128)(2,1)S(1)}, bf16[656,256]{1,0:T(8,128)(2,1)S(1)}, u32[]{:S(2)}, u32[]{:S(2)}) %collective-permute-start.2) | collective-permute-done | bytes 335904 | tf_op jit(solution)/shard_map/ppermute | solution.py:373
  15.0 4.6 %collective-permute-start.3 = (bf16[784,256]{1,0:T(8,128)(2,1)S(1)}, bf16[784,256]{1,0:T(8,128)(2,1)S(1)}, u32[]{:S(2)}, u32[]{:S(2)}) collective-permute-start(bf16[784,256]{1,0:T(8,128)(2,1)S(1)} %shard_map.68), channel_id=1, source_target_pairs={{0,8},{8,0},{16,24},{24,16},{32,40},{40,32},{48,56},{56,48},{64,72... | collective-permute-start | bytes 1204232 | tf_op jit(solution)/shard_map/ppermute | solution.py:388
  19.6 1.0 %collective-permute-done.far_ref.k2_ref = bf16[512,256]{1,0:T(8,128)(2,1)S(1)} collective-permute-done((bf16[512,256]{1,0:T(8,128)(2,1)S(1)}, bf16[512,256]{1,0:T(8,128)(2,1)S(1)}, u32[]{:S(2)}, u32[]{:S(2)}) %collective-permute-start) | collective-permute-done | bytes 262176 | tf_op jit(solution)/shard_map/ppermute | solution.py:371
  20.6 0.0 copy-start
  20.6 3.6 %collective-permute-start.1 = (bf16[640,256]{1,0:T(8,128)(2,1)S(1)}, bf16[640,256]{1,0:T(8,128)(2,1)S(1)}, u32[]{:S(2)}, u32[]{:S(2)}) collective-permute-start(bf16[640,256]{1,0:T(8,128)(2,1)S(1)} %shard_map.64), channel_id=1, source_target_pairs={{0,8},{8,0},{16,24},{24,16},{32,40},{40,32},{48,56},{56,48},{64,72... | collective-permute-start | bytes 983048 | tf_op jit(solution)/shard_map/ppermute | solution.py:378
  24.3 5.9 %collective-permute-start.4 = (bf16[256,256]{1,0:T(8,128)(2,1)S(1)}, bf16[256,256]{1,0:T(8,128)(2,1)S(1)}, u32[]{:S(2)}, u32[]{:S(2)}) collective-permute-start(bf16[256,256]{1,0:T(8,128)(2,1)S(1)} %pad_maximum_fusion.1), channel_id=1, source_target_pairs={{8,32},{24,48},{40,64},{56,80},{72,96},{88,112},{104,128},{120,144... | collective-permute-start | bytes 393224 | tf_op jit(solution)/shard_map/ppermute | solution.py:375
  30.1 0.8 %shard_map.65 = (f32[512,256]{1,0:T(8,128)S(1)}, f32[512,256]{1,0:T(8,128)S(1)}, f32[512,256]{1,0:T(8,128)S(1)}) custom-call(bf16[512,256]{1,0:T(8,128)(2,1)S(1)} %copy-done, bf16[512,256]{1,0:T(8,128)(2,1)S(1)} %copy-done.1, bf16[656,256]{1,0:T(8,128)(2,1)S(1)} %pad_maximum_fusion.v_ref.own_ref), custom_call_target="tpu_custom_call" | custom-call | flops 314572800 | bytes 2433024 | tf_op jit(solution)/shard_map/pallas_call | solution.py:346
  31.0 0.0 collective-permute-done.1.k1_ref
  31.0 0.0 copy-start.2
  31.0 1.3 %shard_map.66 = (bf16[512,1024]{1,0:T(8,128)(2,1)S(1)}, bf16[512,1024]{1,0:T(8,128)(2,1)S(1)}, f32[512,256]{1,0:T(8,128)S(1)}, f32[512,256]{1,0:T(8,128)S(1)}) custom-call(bf16[512,256]{1,0:T(8,128)(2,1)S(1)} %copy-done, bf16[512,256]{1,0:T(8,128)(2,1)S(1)} %collective-permute-done.far_ref.k2_ref, bf16[640,256]{1,0:T(8,128)(2,1)S(1)} %collective-permute-done.1.k1_ref, ...), custom_call_target="tpu_custom_call" | custom-call | flops 419430400 | bytes 5046272 | tf_op jit(solution)/shard_map/pallas_call | solution.py:346
  32.4 0.0 copy-start.3
  32.4 0.0 copy-start.4
  32.4 0.7 %copy-done.3 = bf16[128,16]{0,1:T(8,128)(2,1)S(1)} copy-done((bf16[128,16]{0,1:T(8,128)(2,1)S(1)}, bf16[128,16]{0,1:T(8,128)(2,1)}, u32[]{:S(2)}) %copy-start.3) | copy-done | bytes 4120
  33.0 0.0 copy-done.4
  33.1 0.7 %shard_map.67 = (f32[512,256]{1,0:T(8,128)S(1)}, bf16[2048,256]{1,0:T(8,128)(2,1)S(1)}, f32[16,256]{1,0:T(8,128)S(1)}) custom-call(bf16[512,1024]{1,0:T(8,128)(2,1)S(1)} %get-tuple-element.22.far_ref, f32[512,256]{1,0:T(8,128)S(1)} %get-tuple-element.23.shrink_ref, f32[512,256]{1,0:T(8,128)S(1)} %get-tuple-element.24.acc_ref, ...), custom_call_target="tpu_custom_call" | custom-call | flops 209715200 | bytes 4036608 | tf_op jit(solution)/shard_map/pallas_call | solution.py:346
  33.8 0.0 collective-permute-done.4.tails_ref
  33.8 0.0 collective-permute-done.3.v1_ref
  33.8 1.5 %shard_map.69 = (bf16[512,256]{1,0:T(8,128)(2,1)S(1)}, bf16[144,256]{1,0:T(8,128)(2,1)S(1)}, f32[8,1,768]{2,1,0:T(1,128)S(1)}) custom-call(bf16[512,1024]{1,0:T(8,128)(2,1)S(1)} %get-tuple-element.20.near_ref, f32[512,256]{1,0:T(8,128)S(1)} %get-tuple-element.21.inv_ref, f32[512,256]{1,0:T(8,128)S(1)} %get-tuple-element.25.acc_ref, ...), custom_call_target="tpu_custom_call" | custom-call | flops 524288000 | bytes 3915776 | tf_op jit(solution)/shard_map/pallas_call | solution.py:346
  35.3 10.0 %all_to_all.5.sq_ref = f32[8,1,768]{2,1,0:T(1,128)S(1)} all-to-all(f32[8,1,768]{2,1,0:T(1,128)S(1)} %get-tuple-element.26), channel_id=1, replica_groups=mesh['ctx'=128,'fsdp'=8] {'fsdp'}, dimensions={0} | all-to-all | bytes 49152 | tf_op jit(solution)/shard_map/all_to_all | solution.py:402
  45.3 2.5 %shard_map.70 = bf16[512,256]{1,0:T(8,128)(2,1)} custom-call(f32[8,1,768]{2,1,0:T(1,128)S(1)} %all_to_all.5.sq_ref, bf16[144,256]{1,0:T(8,128)(2,1)S(1)} %get-tuple-element.27.halo_ref, bf16[512,256]{1,0:T(8,128)(2,1)S(1)} %get-tuple-element.28.att_ref, f32[16,256]{1,0:T(8,128)S(1)} %get-tuple-element.29.coef_ref, ...), custom_call_target="tpu_custom_call" | custom-call | flops 1073741824 | bytes 1687552 | tf_op jit(solution)/shard_map/pallas_call | solution.py:346
  (11 shorter events, 0.1 us)
Async XLA Ops:
  0.0 0.9 %slice-start = ((bf16[512,256]{1,0:T(8,128)(2,1)}), bf16[144,256]{1,0:T(8,128)(2,1)S(1)}, s32[]{:S(2)}) async-start(bf16[512,256]{1,0:T(8,128)(2,1)} %q_ref.3), calls=%async_computation.1 | async-start | bytes 147456 | tf_op jit(solution)/shard_map/slice | solution.py:372
  0.9 5.7 %copy-start.1 = (bf16[512,256]{1,0:T(8,128)(2,1)S(1)}, bf16[512,256]{1,0:T(8,128)(2,1)}, u32[]{:S(2)}) copy-start(bf16[512,256]{1,0:T(8,128)(2,1)} %k_ref.1) | copy-start | bytes 786436
  1.9 13.1 %collective-permute-start.2 = (bf16[656,256]{1,0:T(8,128)(2,1)S(1)}, bf16[656,256]{1,0:T(8,128)(2,1)S(1)}, u32[]{:S(2)}, u32[]{:S(2)}) collective-permute-start(bf16[656,256]{1,0:T(8,128)(2,1)S(1)} %pad_maximum_fusion.v_ref.own_ref), channel_id=1, source_target_pairs={{0,16},{8,24},{16,32},{24,40},{32,48},{40,56},{48,64},{56,72},{64,... | collective-permute-start | bytes 1007624 | tf_op jit(solution)/shard_map/ppermute | solution.py:373
  6.6 14.0 %collective-permute-start = (bf16[512,256]{1,0:T(8,128)(2,1)S(1)}, bf16[512,256]{1,0:T(8,128)(2,1)S(1)}, u32[]{:S(2)}, u32[]{:S(2)}) collective-permute-start(bf16[512,256]{1,0:T(8,128)(2,1)S(1)} %copy-done.1), channel_id=1, source_target_pairs={{0,16},{8,24},{16,32},{24,40},{32,48},{40,56},{48,64},{56,72},{64,... | collective-permute-start | bytes 786440 | tf_op jit(solution)/shard_map/ppermute | solution.py:371
  15.0 18.8 %collective-permute-start.3 = (bf16[784,256]{1,0:T(8,128)(2,1)S(1)}, bf16[784,256]{1,0:T(8,128)(2,1)S(1)}, u32[]{:S(2)}, u32[]{:S(2)}) collective-permute-start(bf16[784,256]{1,0:T(8,128)(2,1)S(1)} %shard_map.68), channel_id=1, source_target_pairs={{0,8},{8,0},{16,24},{24,16},{32,40},{40,32},{48,56},{56,48},{64,72... | collective-permute-start | bytes 1204232 | tf_op jit(solution)/shard_map/ppermute | solution.py:388
  20.6 3.6 %slice-start.1 = ((bf16[512,256]{1,0:T(8,128)(2,1)}), bf16[128,256]{1,0:T(8,128)(2,1)S(1)}, s32[]{:S(2)}) async-start(bf16[512,256]{1,0:T(8,128)(2,1)} %param.8), calls=%async_computation.2 | async-start | bytes 131072 | tf_op jit(solution)/shard_map/slice | solution.py:374
  20.6 9.5 %copy-start = (bf16[512,256]{1,0:T(8,128)(2,1)S(1)}, bf16[512,256]{1,0:T(8,128)(2,1)}, u32[]{:S(2)}) copy-start(bf16[512,256]{1,0:T(8,128)(2,1)} %q_ref.3) | copy-start | bytes 786436
  20.6 10.4 %collective-permute-start.1 = (bf16[640,256]{1,0:T(8,128)(2,1)S(1)}, bf16[640,256]{1,0:T(8,128)(2,1)S(1)}, u32[]{:S(2)}, u32[]{:S(2)}) collective-permute-start(bf16[640,256]{1,0:T(8,128)(2,1)S(1)} %shard_map.64), channel_id=1, source_target_pairs={{0,8},{8,0},{16,24},{24,16},{32,40},{40,32},{48,56},{56,48},{64,72... | collective-permute-start | bytes 983048 | tf_op jit(solution)/shard_map/ppermute | solution.py:378
  24.3 9.5 %collective-permute-start.4 = (bf16[256,256]{1,0:T(8,128)(2,1)S(1)}, bf16[256,256]{1,0:T(8,128)(2,1)S(1)}, u32[]{:S(2)}, u32[]{:S(2)}) collective-permute-start(bf16[256,256]{1,0:T(8,128)(2,1)S(1)} %pad_maximum_fusion.1), channel_id=1, source_target_pairs={{8,32},{24,48},{40,64},{56,80},{72,96},{88,112},{104,128},{120,144... | collective-permute-start | bytes 393224 | tf_op jit(solution)/shard_map/ppermute | solution.py:375
  31.0 1.4 %copy-start.2 = (f32[3,3,256]{2,1,0:T(4,128)S(1)}, f32[3,3,256]{2,1,0:T(4,128)}, u32[]{:S(2)}) copy-start(f32[3,3,256]{2,1,0:T(4,128)} %short_ref.1) | copy-start | bytes 27652
  32.4 0.7 %copy-start.3 = (bf16[128,16]{0,1:T(8,128)(2,1)S(1)}, bf16[128,16]{0,1:T(8,128)(2,1)}, u32[]{:S(2)}) copy-start(bf16[128,16]{0,1:T(8,128)(2,1)} %param.11) | copy-start | bytes 12292
  32.4 0.7 %copy-start.4 = (f32[256]{0:T(256)S(1)}, f32[256]{0:T(256)}, u32[]{:S(2)}) copy-start(f32[256]{0:T(256)} %param.9) | copy-start | bytes 3076

commit v2 on v1

--- a/solution.py
+++ b/solution.py
@@ -259,22 +259,31 @@
                 preferred_element_type=F32,
             )
             out_ref[part(b), cols] = (total * inv_ref[part(b), cols]).astype(BF16)
+
+    def halo_rows(h, ahead):
+        att = finish(weigh(units[h], *ahead))
+        halo_out[:, cols_of(h)] = jnp.where(
+            lax.axis_index("ctx") >= 1, att, jnp.zeros(att.shape, BF16)
+        )
+
+    ahead = peak_of(units[0])
+    for h in range(heads):
+        now = ahead
+        if h + 1 < heads:
+            ahead = peak_of(units[h + 1])
+        if h < blocks:
+            main(h)
+        halo_rows(h, now)
+    for b in range(heads, blocks):
+        main(b)
+    for b in range(blocks):
         sq_ref[:, 0, part(b + 1)] = row_squares(out_ref[part(b), :])
-
-    ahead = [peak_of(unit) for unit in units]
-    for i in range(max(heads, blocks)):
-        if i < blocks:
-            main(i)
-        if i < heads:
-            att = finish(weigh(units[i], *ahead[i]))
-            halo_out[:, cols_of(i)] = jnp.where(
-                lax.axis_index("ctx") >= 1, att, jnp.zeros(att.shape, BF16)
-            )
     sq_ref[:, 0, :HALO] = row_squares(halo_out[...])
 
 
 def mix_kernel(
-    total_channels, sq_ref, halo_ref, att_ref, coef_ref, table_ref, out_ref, ext_ref, prod_ref, query_ref
+    total_channels, sq_ref, halo_ref, att_ref, coef_ref, table_ref, out_ref, ext_ref, prod_ref, query_ref,
+    mixed_ref, sems,
 ):
     rows, channels = att_ref.shape
     taps = table_ref.shape[1] // 2
@@ -316,10 +325,11 @@
                 query_ref[r - taps : r, lanes] = branch[0]
     group = lax.broadcasted_iota(jnp.int32, (taps, 128), 1) // (128 // per_lane_tile)
     n = taps * per_lane_tile
-    for w in range(0, channels, 128):
-        lanes = slice(w, w + 128)
-        at = (w // 128) * n
-        for r in range(0, rows, 2 * taps):
+    copies = []
+    for r in range(0, rows, 2 * taps):
+        for w in range(0, channels, 128):
+            lanes = slice(w, w + 128)
+            at = (w // 128) * n
             pair = jnp.concatenate(
                 [prod_ref[r + d : r + d + 2 * taps, lanes] for d in (0, taps)], axis=1
             )
@@ -331,23 +341,31 @@
                     long_mix = jnp.where(
                         group == g, mixed[g * taps : (g + 1) * taps, i * 128 : (i + 1) * 128], long_mix
                     )
-                out_ref[ri : ri + taps, lanes] = (
-                    att_ref[ri : ri + taps, lanes].astype(F32) + query_ref[ri : ri + taps, lanes] * long_mix
+                mixed_ref[ri : ri + taps, lanes] = (
+                    att_ref[ri : ri + taps, lanes].astype(F32)
+                    + query_ref[ri : ri + taps, lanes] * long_mix
                 ).astype(BF16)
+        at = slice(r, r + 2 * taps)
+        copies.append(
+            pltpu.make_async_copy(mixed_ref.at[at, :], out_ref.at[at, :], sems.at[len(copies)])
+        )
+        copies[-1].start()
+    for copy in copies:
+        copy.wait()
 
 
 def array(*dims, dtype=BF16):
     return jax.ShapeDtypeStruct(dims, dtype)
 
 
-def call(kernel, out_shape, args, scratch=(), flops=0, mib=8, spec=VMEM):
+def call(kernel, out_shape, args, scratch=(), flops=0, mib=8, out_spec=VMEM):
     outs = out_shape if isinstance(out_shape, tuple) else (out_shape,)
     nbytes = sum(math.prod(a.shape) * a.dtype.itemsize for a in (*args, *outs))
     result = pl.pallas_call(
         kernel,
         out_shape=outs,
-        in_specs=[spec] * len(args),
-        out_specs=tuple(VMEM for _ in outs),
+        in_specs=[VMEM] * len(args),
+        out_specs=tuple(out_spec for _ in outs),
         scratch_shapes=list(scratch),
         cost_estimate=pl.CostEstimate(flops=flops, bytes_accessed=nbytes, transcendentals=0),
         compiler_params=pltpu.CompilerParams(vmem_limit_bytes=mib << 20),
@@ -407,8 +425,10 @@
             pltpu.VMEM((rows + HALO, channels), F32),
             pltpu.VMEM((rows + taps, channels), BF16),
             pltpu.VMEM((rows, channels), F32),
+            pltpu.VMEM((rows, channels), BF16),
+            pltpu.SemaphoreType.DMA((2,)),
         ),
-        flops=1 << 30, mib=12,
+        flops=1 << 30, mib=12, out_spec=pl.BlockSpec(memory_space=pl.ANY),
     )
 
 

time: 48.1 us -> 47.9 us (level)
  no operation moved by 1% of the time
where the time goes in v2:
time: 47.9 us; the launch traced here: 47.5 us
  starting transfers between devices  23.4 us (49%)
  blocking collectives  10 us (21%)
  Pallas kernels  6.65 us (14%)
  waiting for transfers between devices  4.7 us (10%)
  local copies, waits for them, and re-layouts  1.58 us (3%)
  other arithmetic  1.03 us (2%)
    all_to_all x1, blocking collectives, per_device(): shared = lax.all_to_all(squares, 'fsdp', 0, 0, tiled=True)  10 us
    pallas_call x7, Pallas kernels, call(): pl.pallas_call(kernel, out_shape=outs, in_specs=[VMEM] * len(args), out_s...  6.65 us
    ppermute x1, starting transfers between devices, per_device(): tails3 = lax.ppermute(tails, 'ctx', behind_three)  5.87 us
    ppermute x1, starting transfers between devices, per_device(): k2 = lax.ppermute(keys, 'ctx', ahead)  4.7 us
    ppermute x1, starting transfers between devices, per_device(): vq2 = lax.ppermute(vq, 'ctx', ahead)  4.65 us
    ppermute x1, starting transfers between devices, per_device(): v1 = lax.ppermute(picked, 'ctx', beside)  4.58 us
    ppermute x1, waiting for transfers between devices, per_device(): vq2 = lax.ppermute(vq, 'ctx', ahead)  3.69 us
    ppermute x1, starting transfers between devices, per_device(): k1 = lax.ppermute(picked, 'ctx', beside)  3.58 us
  transfers between devices with their start and end apart: 5, of which 2 were waited for; matrix products, arithmetic and copies ran while one was open for 0% of the time, Pallas kernels for 6%

profile of v2, /device:TPU:353, one launch (start us, length us, event | category | flops | bytes accessed | tf_op | source)
XLA Modules:
  0.0 47.5 jit_solution(9297578336710253902)
XLA Ops:
  0.0 0.9 %slice-done = bf16[144,256]{1,0:T(8,128)(2,1)S(1)} async-done(((bf16[512,256]{1,0:T(8,128)(2,1)}), bf16[144,256]{1,0:T(8,128)(2,1)S(1)}, s32[]{:S(2)}) %slice-start) | async-done | bytes 73752 | tf_op jit(solution)/shard_map/slice | solution.py:390
  0.9 1.0 %pad_maximum_fusion.v_ref.own_ref = bf16[656,256]{1,0:T(8,128)(2,1)S(1)} fusion(bf16[144,256]{1,0:T(8,128)(2,1)S(1)} %slice-done, bf16[512,256]{1,0:T(8,128)(2,1)} %param.8), kind=kLoop, calls=%fused_computation | loop fusion | flops 671744 | bytes 671744 | tf_op jit(solution)/shard_map/concatenate | solution.py:390
  1.9 4.7 %collective-permute-start.2 = (bf16[656,256]{1,0:T(8,128)(2,1)S(1)}, bf16[656,256]{1,0:T(8,128)(2,1)S(1)}, u32[]{:S(2)}, u32[]{:S(2)}) collective-permute-start(bf16[656,256]{1,0:T(8,128)(2,1)S(1)} %pad_maximum_fusion.v_ref.own_ref), channel_id=1, source_target_pairs={{0,16},{8,24},{16,32},{24,40},{32,48},{40,56},{48,64},{56,72},{64,... | collective-permute-start | bytes 1007624 | tf_op jit(solution)/shard_map/ppermute | solution.py:391
  6.6 4.7 %collective-permute-start = (bf16[512,256]{1,0:T(8,128)(2,1)S(1)}, bf16[512,256]{1,0:T(8,128)(2,1)S(1)}, u32[]{:S(2)}, u32[]{:S(2)}) collective-permute-start(bf16[512,256]{1,0:T(8,128)(2,1)S(1)} %copy-done.1), channel_id=1, source_target_pairs={{0,16},{8,24},{16,32},{24,40},{32,48},{40,56},{48,64},{56,72},{64,... | collective-permute-start | bytes 786440 | tf_op jit(solution)/shard_map/ppermute | solution.py:389
  11.3 3.7 %collective-permute-done.2.v2_ref.far_ref = bf16[656,256]{1,0:T(8,128)(2,1)S(1)} collective-permute-done((bf16[656,256]{1,0:T(8,128)(2,1)S(1)}, bf16[656,256]{1,0:T(8,128)(2,1)S(1)}, u32[]{:S(2)}, u32[]{:S(2)}) %collective-permute-start.2) | collective-permute-done | bytes 335904 | tf_op jit(solution)/shard_map/ppermute | solution.py:391
  15.0 4.6 %collective-permute-start.3 = (bf16[784,256]{1,0:T(8,128)(2,1)S(1)}, bf16[784,256]{1,0:T(8,128)(2,1)S(1)}, u32[]{:S(2)}, u32[]{:S(2)}) collective-permute-start(bf16[784,256]{1,0:T(8,128)(2,1)S(1)} %shard_map.68), channel_id=1, source_target_pairs={{0,8},{8,0},{16,24},{24,16},{32,40},{40,32},{48,56},{56,48},{64,72... | collective-permute-start | bytes 1204232 | tf_op jit(solution)/shard_map/ppermute | solution.py:406
  19.6 1.0 %collective-permute-done.far_ref.k2_ref = bf16[512,256]{1,0:T(8,128)(2,1)S(1)} collective-permute-done((bf16[512,256]{1,0:T(8,128)(2,1)S(1)}, bf16[512,256]{1,0:T(8,128)(2,1)S(1)}, u32[]{:S(2)}, u32[]{:S(2)}) %collective-permute-start) | collective-permute-done | bytes 262176 | tf_op jit(solution)/shard_map/ppermute | solution.py:389
  20.6 0.0 copy-start
  20.6 3.6 %collective-permute-start.1 = (bf16[640,256]{1,0:T(8,128)(2,1)S(1)}, bf16[640,256]{1,0:T(8,128)(2,1)S(1)}, u32[]{:S(2)}, u32[]{:S(2)}) collective-permute-start(bf16[640,256]{1,0:T(8,128)(2,1)S(1)} %shard_map.64), channel_id=1, source_target_pairs={{0,8},{8,0},{16,24},{24,16},{32,40},{40,32},{48,56},{56,48},{64,72... | collective-permute-start | bytes 983048 | tf_op jit(solution)/shard_map/ppermute | solution.py:396
  24.3 5.9 %collective-permute-start.4 = (bf16[256,256]{1,0:T(8,128)(2,1)S(1)}, bf16[256,256]{1,0:T(8,128)(2,1)S(1)}, u32[]{:S(2)}, u32[]{:S(2)}) collective-permute-start(bf16[256,256]{1,0:T(8,128)(2,1)S(1)} %pad_maximum_fusion.1), channel_id=1, source_target_pairs={{8,32},{24,48},{40,64},{56,80},{72,96},{88,112},{104,128},{120,144... | collective-permute-start | bytes 393224 | tf_op jit(solution)/shard_map/ppermute | solution.py:393
  30.1 0.8 %shard_map.65 = (f32[512,256]{1,0:T(8,128)S(1)}, f32[512,256]{1,0:T(8,128)S(1)}, f32[512,256]{1,0:T(8,128)S(1)}) custom-call(bf16[512,256]{1,0:T(8,128)(2,1)S(1)} %copy-done, bf16[512,256]{1,0:T(8,128)(2,1)S(1)} %copy-done.1, bf16[656,256]{1,0:T(8,128)(2,1)S(1)} %pad_maximum_fusion.v_ref.own_ref), custom_call_target="tpu_custom_call" | custom-call | flops 314572800 | bytes 2433024 | tf_op jit(solution)/shard_map/pallas_call | solution.py:364
  31.0 0.0 collective-permute-done.1.k1_ref
  31.0 0.0 copy-start.2
  31.0 1.3 %shard_map.66 = (bf16[512,1024]{1,0:T(8,128)(2,1)S(1)}, bf16[512,1024]{1,0:T(8,128)(2,1)S(1)}, f32[512,256]{1,0:T(8,128)S(1)}, f32[512,256]{1,0:T(8,128)S(1)}) custom-call(bf16[512,256]{1,0:T(8,128)(2,1)S(1)} %copy-done, bf16[512,256]{1,0:T(8,128)(2,1)S(1)} %collective-permute-done.far_ref.k2_ref, bf16[640,256]{1,0:T(8,128)(2,1)S(1)} %collective-permute-done.1.k1_ref, ...), custom_call_target="tpu_custom_call" | custom-call | flops 419430400 | bytes 5046272 | tf_op jit(solution)/shard_map/pallas_call | solution.py:364
  32.4 0.0 copy-start.3
  32.4 0.0 copy-start.4
  32.4 0.7 %copy-done.3 = bf16[128,16]{0,1:T(8,128)(2,1)S(1)} copy-done((bf16[128,16]{0,1:T(8,128)(2,1)S(1)}, bf16[128,16]{0,1:T(8,128)(2,1)}, u32[]{:S(2)}) %copy-start.3) | copy-done | bytes 4120
  33.0 0.0 copy-done.4
  33.1 0.7 %shard_map.67 = (f32[512,256]{1,0:T(8,128)S(1)}, bf16[2048,256]{1,0:T(8,128)(2,1)S(1)}, f32[16,256]{1,0:T(8,128)S(1)}) custom-call(bf16[512,1024]{1,0:T(8,128)(2,1)S(1)} %get-tuple-element.22.far_ref, f32[512,256]{1,0:T(8,128)S(1)} %get-tuple-element.23.shrink_ref, f32[512,256]{1,0:T(8,128)S(1)} %get-tuple-element.24.acc_ref, ...), custom_call_target="tpu_custom_call" | custom-call | flops 209715200 | bytes 4036608 | tf_op jit(solution)/shard_map/pallas_call | solution.py:364
  33.8 0.0 collective-permute-done.4.tails_ref
  33.8 0.0 collective-permute-done.3.v1_ref
  33.8 1.3 %shard_map.69 = (bf16[512,256]{1,0:T(8,128)(2,1)S(1)}, bf16[144,256]{1,0:T(8,128)(2,1)S(1)}, f32[8,1,768]{2,1,0:T(1,128)S(1)}) custom-call(bf16[512,1024]{1,0:T(8,128)(2,1)S(1)} %get-tuple-element.20.near_ref, f32[512,256]{1,0:T(8,128)S(1)} %get-tuple-element.21.inv_ref, f32[512,256]{1,0:T(8,128)S(1)} %get-tuple-element.25.acc_ref, ...), custom_call_target="tpu_custom_call" | custom-call | flops 524288000 | bytes 3915776 | tf_op jit(solution)/shard_map/pallas_call | solution.py:364
  35.1 10.0 %all_to_all.5.sq_ref = f32[8,1,768]{2,1,0:T(1,128)S(1)} all-to-all(f32[8,1,768]{2,1,0:T(1,128)S(1)} %get-tuple-element.26), channel_id=1, replica_groups=mesh['ctx'=128,'fsdp'=8] {'fsdp'}, dimensions={0} | all-to-all | bytes 49152 | tf_op jit(solution)/shard_map/all_to_all | solution.py:420
  45.1 2.4 %shard_map.70 = bf16[512,256]{1,0:T(8,128)(2,1)} custom-call(f32[8,1,768]{2,1,0:T(1,128)S(1)} %all_to_all.5.sq_ref, bf16[144,256]{1,0:T(8,128)(2,1)S(1)} %get-tuple-element.27.halo_ref, bf16[512,256]{1,0:T(8,128)(2,1)S(1)} %get-tuple-element.28.att_ref, f32[16,256]{1,0:T(8,128)S(1)} %get-tuple-element.29.coef_ref, ...), custom_call_target="tpu_custom_call" | custom-call | flops 1073741824 | bytes 1687552 | tf_op jit(solution)/shard_map/pallas_call | solution.py:364
  (11 shorter events, 0.1 us)
Async XLA Ops:
  0.0 0.9 %slice-start = ((bf16[512,256]{1,0:T(8,128)(2,1)}), bf16[144,256]{1,0:T(8,128)(2,1)S(1)}, s32[]{:S(2)}) async-start(bf16[512,256]{1,0:T(8,128)(2,1)} %q_ref.3), calls=%async_computation.1 | async-start | bytes 147456 | tf_op jit(solution)/shard_map/slice | solution.py:390
  0.9 5.7 %copy-start.1 = (bf16[512,256]{1,0:T(8,128)(2,1)S(1)}, bf16[512,256]{1,0:T(8,128)(2,1)}, u32[]{:S(2)}) copy-start(bf16[512,256]{1,0:T(8,128)(2,1)} %k_ref.1) | copy-start | bytes 786436
  1.9 13.1 %collective-permute-start.2 = (bf16[656,256]{1,0:T(8,128)(2,1)S(1)}, bf16[656,256]{1,0:T(8,128)(2,1)S(1)}, u32[]{:S(2)}, u32[]{:S(2)}) collective-permute-start(bf16[656,256]{1,0:T(8,128)(2,1)S(1)} %pad_maximum_fusion.v_ref.own_ref), channel_id=1, source_target_pairs={{0,16},{8,24},{16,32},{24,40},{32,48},{40,56},{48,64},{56,72},{64,... | collective-permute-start | bytes 1007624 | tf_op jit(solution)/shard_map/ppermute | solution.py:391
  6.6 14.0 %collective-permute-start = (bf16[512,256]{1,0:T(8,128)(2,1)S(1)}, bf16[512,256]{1,0:T(8,128)(2,1)S(1)}, u32[]{:S(2)}, u32[]{:S(2)}) collective-permute-start(bf16[512,256]{1,0:T(8,128)(2,1)S(1)} %copy-done.1), channel_id=1, source_target_pairs={{0,16},{8,24},{16,32},{24,40},{32,48},{40,56},{48,64},{56,72},{64,... | collective-permute-start | bytes 786440 | tf_op jit(solution)/shard_map/ppermute | solution.py:389
  15.0 18.8 %collective-permute-start.3 = (bf16[784,256]{1,0:T(8,128)(2,1)S(1)}, bf16[784,256]{1,0:T(8,128)(2,1)S(1)}, u32[]{:S(2)}, u32[]{:S(2)}) collective-permute-start(bf16[784,256]{1,0:T(8,128)(2,1)S(1)} %shard_map.68), channel_id=1, source_target_pairs={{0,8},{8,0},{16,24},{24,16},{32,40},{40,32},{48,56},{56,48},{64,72... | collective-permute-start | bytes 1204232 | tf_op jit(solution)/shard_map/ppermute | solution.py:406
  20.6 3.6 %slice-start.1 = ((bf16[512,256]{1,0:T(8,128)(2,1)}), bf16[128,256]{1,0:T(8,128)(2,1)S(1)}, s32[]{:S(2)}) async-start(bf16[512,256]{1,0:T(8,128)(2,1)} %param.8), calls=%async_computation.2 | async-start | bytes 131072 | tf_op jit(solution)/shard_map/slice | solution.py:392
  20.6 9.5 %copy-start = (bf16[512,256]{1,0:T(8,128)(2,1)S(1)}, bf16[512,256]{1,0:T(8,128)(2,1)}, u32[]{:S(2)}) copy-start(bf16[512,256]{1,0:T(8,128)(2,1)} %q_ref.3) | copy-start | bytes 786436
  20.6 10.4 %collective-permute-start.1 = (bf16[640,256]{1,0:T(8,128)(2,1)S(1)}, bf16[640,256]{1,0:T(8,128)(2,1)S(1)}, u32[]{:S(2)}, u32[]{:S(2)}) collective-permute-start(bf16[640,256]{1,0:T(8,128)(2,1)S(1)} %shard_map.64), channel_id=1, source_target_pairs={{0,8},{8,0},{16,24},{24,16},{32,40},{40,32},{48,56},{56,48},{64,72... | collective-permute-start | bytes 983048 | tf_op jit(solution)/shard_map/ppermute | solution.py:396
  24.3 9.5 %collective-permute-start.4 = (bf16[256,256]{1,0:T(8,128)(2,1)S(1)}, bf16[256,256]{1,0:T(8,128)(2,1)S(1)}, u32[]{:S(2)}, u32[]{:S(2)}) collective-permute-start(bf16[256,256]{1,0:T(8,128)(2,1)S(1)} %pad_maximum_fusion.1), channel_id=1, source_target_pairs={{8,32},{24,48},{40,64},{56,80},{72,96},{88,112},{104,128},{120,144... | collective-permute-start | bytes 393224 | tf_op jit(solution)/shard_map/ppermute | solution.py:393
  31.0 1.4 %copy-start.2 = (f32[3,3,256]{2,1,0:T(4,128)S(1)}, f32[3,3,256]{2,1,0:T(4,128)}, u32[]{:S(2)}) copy-start(f32[3,3,256]{2,1,0:T(4,128)} %short_ref.1) | copy-start | bytes 27652
  32.4 0.7 %copy-start.3 = (bf16[128,16]{0,1:T(8,128)(2,1)S(1)}, bf16[128,16]{0,1:T(8,128)(2,1)}, u32[]{:S(2)}) copy-start(bf16[128,16]{0,1:T(8,128)(2,1)} %param.11) | copy-start | bytes 12292
  32.4 0.7 %copy-start.4 = (f32[256]{0:T(256)S(1)}, f32[256]{0:T(256)}, u32[]{:S(2)}) copy-start(f32[256]{0:T(256)} %param.9) | copy-start | bytes 3076

commit v3 on v2

--- a/solution.py
+++ b/solution.py
@@ -294,13 +294,14 @@
     rest = inverse - high.astype(F32)
     middle = rest.astype(BF16)
     low = (rest - middle.astype(F32)).astype(BF16)
-    first = lax.broadcasted_iota(jnp.int32, (8, 128), 0) == 0
-    ones = jnp.where(first, 1.0, 0.0).astype(BF16)
-    dims = (((0,), (0,)), ((), ()))
-    columns = (
-        lax.dot_general(high, ones, dims, preferred_element_type=F32)
-        + lax.dot_general(middle, ones, dims, preferred_element_type=F32)
-    ) + lax.dot_general(low, ones, dims, preferred_element_type=F32)
+    row = lax.broadcasted_iota(jnp.int32, inverse.shape, 0)
+    terms = jnp.where(
+        row == 0, high.astype(F32), jnp.where(row == 1, middle.astype(F32), low.astype(F32))
+    ).astype(BF16)
+    ones = jnp.where(lax.broadcasted_iota(jnp.int32, (8, 128), 0) < 3, 1.0, 0.0).astype(BF16)
+    columns = lax.dot_general(
+        terms, ones, (((0,), (0,)), ((), ())), preferred_element_type=F32
+    )
     for ref, at, size, start in ((halo_ref, 0, HALO, 0), (att_ref, HALO, rows, BLOCK)):
         for w in range(0, channels, 128):
             lanes = slice(w, w + 128)

time: 47.9 us -> 47.6 us (level)
  the two profiles are of different devices: /device:TPU:353 before, /device:TPU:97 now
where the time goes in v3:
time: 47.6 us; the launch traced here: 47.2 us
  starting transfers between devices  23.4 us (49%)
  blocking collectives  10 us (21%)
  Pallas kernels  6.34 us (13%)
  waiting for transfers between devices  4.7 us (10%)
  local copies, waits for them, and re-layouts  1.58 us (3%)
  other arithmetic  1.03 us (2%)
    all_to_all x1, blocking collectives, per_device(): shared = lax.all_to_all(squares, 'fsdp', 0, 0, tiled=True)  10 us
    pallas_call x7, Pallas kernels, call(): pl.pallas_call(kernel, out_shape=outs, in_specs=[VMEM] * len(args), out_s...  6.34 us
    ppermute x1, starting transfers between devices, per_device(): tails3 = lax.ppermute(tails, 'ctx', behind_three)  5.87 us
    ppermute x1, starting transfers between devices, per_device(): k2 = lax.ppermute(keys, 'ctx', ahead)  4.7 us
    ppermute x1, starting transfers between devices, per_device(): vq2 = lax.ppermute(vq, 'ctx', ahead)  4.65 us
    ppermute x1, starting transfers between devices, per_device(): v1 = lax.ppermute(picked, 'ctx', beside)  4.58 us
    ppermute x1, waiting for transfers between devices, per_device(): vq2 = lax.ppermute(vq, 'ctx', ahead)  3.69 us
    ppermute x1, starting transfers between devices, per_device(): k1 = lax.ppermute(picked, 'ctx', beside)  3.58 us
  transfers between devices with their start and end apart: 5, of which 2 were waited for; matrix products, arithmetic and copies ran while one was open for 0% of the time, Pallas kernels for 6%

profile of v3, /device:TPU:97, one launch (start us, length us, event | category | flops | bytes accessed | tf_op | source)
XLA Modules:
  0.0 47.2 jit_solution(4743752366916349319)
XLA Ops:
  0.0 0.9 %slice-done = bf16[144,256]{1,0:T(8,128)(2,1)S(1)} async-done(((bf16[512,256]{1,0:T(8,128)(2,1)}), bf16[144,256]{1,0:T(8,128)(2,1)S(1)}, s32[]{:S(2)}) %slice-start) | async-done | bytes 73752 | tf_op jit(solution)/shard_map/slice | solution.py:391
  0.9 1.0 %pad_maximum_fusion.v_ref.own_ref = bf16[656,256]{1,0:T(8,128)(2,1)S(1)} fusion(bf16[144,256]{1,0:T(8,128)(2,1)S(1)} %slice-done, bf16[512,256]{1,0:T(8,128)(2,1)} %param.8), kind=kLoop, calls=%fused_computation | loop fusion | flops 671744 | bytes 671744 | tf_op jit(solution)/shard_map/concatenate | solution.py:391
  1.9 4.7 %collective-permute-start.2 = (bf16[656,256]{1,0:T(8,128)(2,1)S(1)}, bf16[656,256]{1,0:T(8,128)(2,1)S(1)}, u32[]{:S(2)}, u32[]{:S(2)}) collective-permute-start(bf16[656,256]{1,0:T(8,128)(2,1)S(1)} %pad_maximum_fusion.v_ref.own_ref), channel_id=1, source_target_pairs={{0,16},{8,24},{16,32},{24,40},{32,48},{40,56},{48,64},{56,72},{64,... | collective-permute-start | bytes 1007624 | tf_op jit(solution)/shard_map/ppermute | solution.py:392
  6.6 4.7 %collective-permute-start = (bf16[512,256]{1,0:T(8,128)(2,1)S(1)}, bf16[512,256]{1,0:T(8,128)(2,1)S(1)}, u32[]{:S(2)}, u32[]{:S(2)}) collective-permute-start(bf16[512,256]{1,0:T(8,128)(2,1)S(1)} %copy-done.1), channel_id=1, source_target_pairs={{0,16},{8,24},{16,32},{24,40},{32,48},{40,56},{48,64},{56,72},{64,... | collective-permute-start | bytes 786440 | tf_op jit(solution)/shard_map/ppermute | solution.py:390
  11.3 3.7 %collective-permute-done.2.v2_ref.far_ref = bf16[656,256]{1,0:T(8,128)(2,1)S(1)} collective-permute-done((bf16[656,256]{1,0:T(8,128)(2,1)S(1)}, bf16[656,256]{1,0:T(8,128)(2,1)S(1)}, u32[]{:S(2)}, u32[]{:S(2)}) %collective-permute-start.2) | collective-permute-done | bytes 335904 | tf_op jit(solution)/shard_map/ppermute | solution.py:392
  15.0 4.6 %collective-permute-start.3 = (bf16[784,256]{1,0:T(8,128)(2,1)S(1)}, bf16[784,256]{1,0:T(8,128)(2,1)S(1)}, u32[]{:S(2)}, u32[]{:S(2)}) collective-permute-start(bf16[784,256]{1,0:T(8,128)(2,1)S(1)} %shard_map.68), channel_id=1, source_target_pairs={{0,8},{8,0},{16,24},{24,16},{32,40},{40,32},{48,56},{56,48},{64,72... | collective-permute-start | bytes 1204232 | tf_op jit(solution)/shard_map/ppermute | solution.py:407
  19.6 1.0 %collective-permute-done.far_ref.k2_ref = bf16[512,256]{1,0:T(8,128)(2,1)S(1)} collective-permute-done((bf16[512,256]{1,0:T(8,128)(2,1)S(1)}, bf16[512,256]{1,0:T(8,128)(2,1)S(1)}, u32[]{:S(2)}, u32[]{:S(2)}) %collective-permute-start) | collective-permute-done | bytes 262176 | tf_op jit(solution)/shard_map/ppermute | solution.py:390
  20.6 0.0 copy-start
  20.6 3.6 %collective-permute-start.1 = (bf16[640,256]{1,0:T(8,128)(2,1)S(1)}, bf16[640,256]{1,0:T(8,128)(2,1)S(1)}, u32[]{:S(2)}, u32[]{:S(2)}) collective-permute-start(bf16[640,256]{1,0:T(8,128)(2,1)S(1)} %shard_map.64), channel_id=1, source_target_pairs={{0,8},{8,0},{16,24},{24,16},{32,40},{40,32},{48,56},{56,48},{64,72... | collective-permute-start | bytes 983048 | tf_op jit(solution)/shard_map/ppermute | solution.py:397
  24.3 5.9 %collective-permute-start.4 = (bf16[256,256]{1,0:T(8,128)(2,1)S(1)}, bf16[256,256]{1,0:T(8,128)(2,1)S(1)}, u32[]{:S(2)}, u32[]{:S(2)}) collective-permute-start(bf16[256,256]{1,0:T(8,128)(2,1)S(1)} %pad_maximum_fusion.1), channel_id=1, source_target_pairs={{8,32},{24,48},{40,64},{56,80},{72,96},{88,112},{104,128},{120,144... | collective-permute-start | bytes 393224 | tf_op jit(solution)/shard_map/ppermute | solution.py:394
  30.1 0.8 %shard_map.65 = (f32[512,256]{1,0:T(8,128)S(1)}, f32[512,256]{1,0:T(8,128)S(1)}, f32[512,256]{1,0:T(8,128)S(1)}) custom-call(bf16[512,256]{1,0:T(8,128)(2,1)S(1)} %copy-done, bf16[512,256]{1,0:T(8,128)(2,1)S(1)} %copy-done.1, bf16[656,256]{1,0:T(8,128)(2,1)S(1)} %pad_maximum_fusion.v_ref.own_ref), custom_call_target="tpu_custom_call" | custom-call | flops 314572800 | bytes 2433024 | tf_op jit(solution)/shard_map/pallas_call | solution.py:365
  31.0 0.0 collective-permute-done.1.k1_ref
  31.0 0.0 copy-start.2
  31.0 1.3 %shard_map.66 = (bf16[512,1024]{1,0:T(8,128)(2,1)S(1)}, bf16[512,1024]{1,0:T(8,128)(2,1)S(1)}, f32[512,256]{1,0:T(8,128)S(1)}, f32[512,256]{1,0:T(8,128)S(1)}) custom-call(bf16[512,256]{1,0:T(8,128)(2,1)S(1)} %copy-done, bf16[512,256]{1,0:T(8,128)(2,1)S(1)} %collective-permute-done.far_ref.k2_ref, bf16[640,256]{1,0:T(8,128)(2,1)S(1)} %collective-permute-done.1.k1_ref, ...), custom_call_target="tpu_custom_call" | custom-call | flops 419430400 | bytes 5046272 | tf_op jit(solution)/shard_map/pallas_call | solution.py:365
  32.4 0.0 copy-start.3
  32.4 0.0 copy-start.4
  32.4 0.7 %copy-done.3 = bf16[128,16]{0,1:T(8,128)(2,1)S(1)} copy-done((bf16[128,16]{0,1:T(8,128)(2,1)S(1)}, bf16[128,16]{0,1:T(8,128)(2,1)}, u32[]{:S(2)}) %copy-start.3) | copy-done | bytes 4120
  33.0 0.0 copy-done.4
  33.1 0.7 %shard_map.67 = (f32[512,256]{1,0:T(8,128)S(1)}, bf16[2048,256]{1,0:T(8,128)(2,1)S(1)}, f32[16,256]{1,0:T(8,128)S(1)}) custom-call(bf16[512,1024]{1,0:T(8,128)(2,1)S(1)} %get-tuple-element.22.far_ref, f32[512,256]{1,0:T(8,128)S(1)} %get-tuple-element.23.shrink_ref, f32[512,256]{1,0:T(8,128)S(1)} %get-tuple-element.24.acc_ref, ...), custom_call_target="tpu_custom_call" | custom-call | flops 209715200 | bytes 4036608 | tf_op jit(solution)/shard_map/pallas_call | solution.py:365
  33.8 0.0 collective-permute-done.4.tails_ref
  33.8 0.0 collective-permute-done.3.v1_ref
  33.8 1.3 %shard_map.69 = (bf16[512,256]{1,0:T(8,128)(2,1)S(1)}, bf16[144,256]{1,0:T(8,128)(2,1)S(1)}, f32[8,1,768]{2,1,0:T(1,128)S(1)}) custom-call(bf16[512,1024]{1,0:T(8,128)(2,1)S(1)} %get-tuple-element.20.near_ref, f32[512,256]{1,0:T(8,128)S(1)} %get-tuple-element.21.inv_ref, f32[512,256]{1,0:T(8,128)S(1)} %get-tuple-element.25.acc_ref, ...), custom_call_target="tpu_custom_call" | custom-call | flops 524288000 | bytes 3915776 | tf_op jit(solution)/shard_map/pallas_call | solution.py:365
  35.1 10.0 %all_to_all.5.sq_ref = f32[8,1,768]{2,1,0:T(1,128)S(1)} all-to-all(f32[8,1,768]{2,1,0:T(1,128)S(1)} %get-tuple-element.26), channel_id=1, replica_groups=mesh['ctx'=128,'fsdp'=8] {'fsdp'}, dimensions={0} | all-to-all | bytes 49152 | tf_op jit(solution)/shard_map/all_to_all | solution.py:421
  45.1 2.1 %shard_map.70 = bf16[512,256]{1,0:T(8,128)(2,1)} custom-call(f32[8,1,768]{2,1,0:T(1,128)S(1)} %all_to_all.5.sq_ref, bf16[144,256]{1,0:T(8,128)(2,1)S(1)} %get-tuple-element.27.halo_ref, bf16[512,256]{1,0:T(8,128)(2,1)S(1)} %get-tuple-element.28.att_ref, f32[16,256]{1,0:T(8,128)S(1)} %get-tuple-element.29.coef_ref, ...), custom_call_target="tpu_custom_call" | custom-call | flops 1073741824 | bytes 1687552 | tf_op jit(solution)/shard_map/pallas_call | solution.py:365
  (11 shorter events, 0.1 us)
Async XLA Ops:
  0.0 0.9 %slice-start = ((bf16[512,256]{1,0:T(8,128)(2,1)}), bf16[144,256]{1,0:T(8,128)(2,1)S(1)}, s32[]{:S(2)}) async-start(bf16[512,256]{1,0:T(8,128)(2,1)} %q_ref.3), calls=%async_computation.1 | async-start | bytes 147456 | tf_op jit(solution)/shard_map/slice | solution.py:391
  0.9 5.7 %copy-start.1 = (bf16[512,256]{1,0:T(8,128)(2,1)S(1)}, bf16[512,256]{1,0:T(8,128)(2,1)}, u32[]{:S(2)}) copy-start(bf16[512,256]{1,0:T(8,128)(2,1)} %k_ref.1) | copy-start | bytes 786436
  1.9 13.1 %collective-permute-start.2 = (bf16[656,256]{1,0:T(8,128)(2,1)S(1)}, bf16[656,256]{1,0:T(8,128)(2,1)S(1)}, u32[]{:S(2)}, u32[]{:S(2)}) collective-permute-start(bf16[656,256]{1,0:T(8,128)(2,1)S(1)} %pad_maximum_fusion.v_ref.own_ref), channel_id=1, source_target_pairs={{0,16},{8,24},{16,32},{24,40},{32,48},{40,56},{48,64},{56,72},{64,... | collective-permute-start | bytes 1007624 | tf_op jit(solution)/shard_map/ppermute | solution.py:392
  6.6 14.0 %collective-permute-start = (bf16[512,256]{1,0:T(8,128)(2,1)S(1)}, bf16[512,256]{1,0:T(8,128)(2,1)S(1)}, u32[]{:S(2)}, u32[]{:S(2)}) collective-permute-start(bf16[512,256]{1,0:T(8,128)(2,1)S(1)} %copy-done.1), channel_id=1, source_target_pairs={{0,16},{8,24},{16,32},{24,40},{32,48},{40,56},{48,64},{56,72},{64,... | collective-permute-start | bytes 786440 | tf_op jit(solution)/shard_map/ppermute | solution.py:390
  15.0 18.8 %collective-permute-start.3 = (bf16[784,256]{1,0:T(8,128)(2,1)S(1)}, bf16[784,256]{1,0:T(8,128)(2,1)S(1)}, u32[]{:S(2)}, u32[]{:S(2)}) collective-permute-start(bf16[784,256]{1,0:T(8,128)(2,1)S(1)} %shard_map.68), channel_id=1, source_target_pairs={{0,8},{8,0},{16,24},{24,16},{32,40},{40,32},{48,56},{56,48},{64,72... | collective-permute-start | bytes 1204232 | tf_op jit(solution)/shard_map/ppermute | solution.py:407
  20.6 3.6 %slice-start.1 = ((bf16[512,256]{1,0:T(8,128)(2,1)}), bf16[128,256]{1,0:T(8,128)(2,1)S(1)}, s32[]{:S(2)}) async-start(bf16[512,256]{1,0:T(8,128)(2,1)} %param.8), calls=%async_computation.2 | async-start | bytes 131072 | tf_op jit(solution)/shard_map/slice | solution.py:393
  20.6 9.5 %copy-start = (bf16[512,256]{1,0:T(8,128)(2,1)S(1)}, bf16[512,256]{1,0:T(8,128)(2,1)}, u32[]{:S(2)}) copy-start(bf16[512,256]{1,0:T(8,128)(2,1)} %q_ref.3) | copy-start | bytes 786436
  20.6 10.4 %collective-permute-start.1 = (bf16[640,256]{1,0:T(8,128)(2,1)S(1)}, bf16[640,256]{1,0:T(8,128)(2,1)S(1)}, u32[]{:S(2)}, u32[]{:S(2)}) collective-permute-start(bf16[640,256]{1,0:T(8,128)(2,1)S(1)} %shard_map.64), channel_id=1, source_target_pairs={{0,8},{8,0},{16,24},{24,16},{32,40},{40,32},{48,56},{56,48},{64,72... | collective-permute-start | bytes 983048 | tf_op jit(solution)/shard_map/ppermute | solution.py:397
  24.3 9.5 %collective-permute-start.4 = (bf16[256,256]{1,0:T(8,128)(2,1)S(1)}, bf16[256,256]{1,0:T(8,128)(2,1)S(1)}, u32[]{:S(2)}, u32[]{:S(2)}) collective-permute-start(bf16[256,256]{1,0:T(8,128)(2,1)S(1)} %pad_maximum_fusion.1), channel_id=1, source_target_pairs={{8,32},{24,48},{40,64},{56,80},{72,96},{88,112},{104,128},{120,144... | collective-permute-start | bytes 393224 | tf_op jit(solution)/shard_map/ppermute | solution.py:394
  31.0 1.4 %copy-start.2 = (f32[3,3,256]{2,1,0:T(4,128)S(1)}, f32[3,3,256]{2,1,0:T(4,128)}, u32[]{:S(2)}) copy-start(f32[3,3,256]{2,1,0:T(4,128)} %short_ref.1) | copy-start | bytes 27652
  32.4 0.7 %copy-start.3 = (bf16[128,16]{0,1:T(8,128)(2,1)S(1)}, bf16[128,16]{0,1:T(8,128)(2,1)}, u32[]{:S(2)}) copy-start(bf16[128,16]{0,1:T(8,128)(2,1)} %param.11) | copy-start | bytes 12292
  32.4 0.7 %copy-start.4 = (f32[256]{0:T(256)S(1)}, f32[256]{0:T(256)}, u32[]{:S(2)}) copy-start(f32[256]{0:T(256)} %param.9) | copy-start | bytes 3076
